TPU v7x, 128 devices: a whole 4x4x4 slice. The times are simulated.
128 devices in a mesh: ctx: 32 (over z, x, core), head: 4 (over y).
Axes of the slice: x: 4, y: 4, z: 4, core: 2. Of those that a mesh axis runs over, the one named last changes fastest.
Arguments:
- queries: bfloat16 [4096, 64, 576], P('ctx', 'head'), may hold values from -104 to 104
- latent: bfloat16 [4096, 576], P('ctx'), may hold values from -6 to 6
- cotangent: bfloat16 [4096, 64, 512], P('ctx', 'head'), may hold values from -6 to 6
- selection: int32 [4096, 32], P('ctx'), may hold values from -1 to 63, as said below
Outputs:
- attended: bfloat16 [4096, 64, 512], P('ctx', 'head')
- grad_queries: bfloat16 [4096, 64, 576], P('ctx', 'head')
- grad_latent: float32 [4096, 576], P('ctx')
Inputs may be any that keep to these rules, and one draw needn't show every extreme that they name: `selection`: row t lists distinct blocks, -1 in unused entries. It always lists the block of token t and never a later block. Call the 128 tokens of one index of the ctx axis a range. Besides blocks of its own range, a row lists at most one block of any other range; that range lies earlier, and all tokens of one 64-token block that list a block of a given range list the same one. So the tokens of one range list at most 2 blocks of another range. Rows of the last range always list a block of the first range. A row has unused entries only where fewer than 32 blocks are allowed by these rules.
All inputs are finite; a program needn't handle non-finite values.
Results may differ from a plain program's by a relative error of at most 0.03.
Values may be sent and summed in bfloat16 or wider, within the bound.
A program may use at most 128 MiB of HBM per device.

v0:
```python
import functools

import jax
import jax.numpy as jnp
from jax import lax
from jax.experimental import pallas as pl
from jax.experimental.pallas import tpu as pltpu
from jax.sharding import PartitionSpec as P

BLOCK = 64
SCALE = 192.0 ** (-0.5)
LOG2E = 1.4426950408889634
BIG = 1e30
PLANE = 8
NT = (((1,), (1,)), ((), ()))
NN = (((1,), (0,)), ((), ()))


def dot(a, b, dims):
    return lax.dot_general(a, b, dims, preferred_element_type=jnp.float32)


def attention_kernel(
    me_ref, wanted, mask, q, do, latent, out, dq, dlat,
    qx, qt, dot_t, ksel, kx, s, p, sx, px, mrow, arow, drow, acc, accx, *, rows,
):
    shard = me_ref[0]
    plane = shard // PLANE
    width = q.shape[1]
    value = do.shape[1]
    half = BLOCK * 16
    keys = PLANE * BLOCK
    pad = qx.shape[1] - width
    c = SCALE * LOG2E

    column = lax.broadcasted_iota(jnp.int32, (BLOCK, pad), 1)

    def pick(j, carry):
        one = jnp.where(column == j, 1.0, 0.0).astype(jnp.bfloat16)
        k0 = latent[pl.ds(pl.multiple_of(j * 128, 128), 64), :]
        k1 = latent[pl.ds(pl.multiple_of(j * 128 + 64, 64), 64), :]
        at = pl.ds(pl.multiple_of(j * 64, 64), 64)
        for b in range(2):
            ksel[b, at, :width] = jnp.where(wanted[b, j] == 1, k1, k0)
            ksel[b, at, width:] = one
        return carry

    lax.fori_loop(0, (plane + 1) * PLANE, pick, 0)
    kx[:, :width] = latent[pl.ds(pl.multiple_of(shard * 128, 128), 64), :]
    kx[:, width:] = jnp.where(column == 32, 1.0, 0.0).astype(jnp.bfloat16)

    qx[:, :width] = q[...]
    qx[:, width:] = jnp.broadcast_to(mask[...][:, None, :], (128, 16, pad)).reshape(2048, pad)
    qt[...] = q[...].T

    lane = lax.broadcasted_iota(jnp.int32, (rows, keys), 1)
    row = lax.broadcasted_iota(jnp.int32, (rows, keys), 0)
    tiles = half // rows

    def row_slice(b, t):
        return pl.ds(pl.multiple_of(b * half + t * rows, rows), rows)

    def scores(g, b, own):
        at = pl.ds(pl.multiple_of(g * keys, keys), keys)

        def tile(t, carry):
            r = row_slice(b, t)
            x = dot(qx[r, :], ksel[b, at, :], NT)
            if own:
                slot = lax.rem(shard, PLANE)
                late = (lane // BLOCK == slot) & (lane % BLOCK > (row + t * rows) // 16)
                x = jnp.where(late, -BIG, x)
            s[g, r, :] = x
            top = jnp.maximum(
                jnp.maximum(x[:, 0:128], x[:, 128:256]), jnp.maximum(x[:, 256:384], x[:, 384:512])
            )
            if own:
                if b == 1:
                    y = dot(qx[r, :], kx[...], NT)
                    sx[pl.ds(pl.multiple_of(t * rows, rows), rows), :] = y
                    top = jnp.maximum(top, jnp.concatenate([y, y], axis=1))
                mrow[r, :] = top
            else:
                mrow[r, :] = jnp.maximum(mrow[r, :], top)
            return carry

        lax.fori_loop(0, tiles, tile, 0)

    scores(plane, 0, True)
    scores(plane, 1, True)

    def score_step(g, carry):
        scores(g, 0, False)
        scores(g, 1, False)
        return carry

    lax.fori_loop(0, plane, score_step, 0)

    for b in range(2):
        def tile(t, carry, b=b):
            r = row_slice(b, t)
            top = jnp.max(mrow[r, :], axis=1, keepdims=True) * c
            if b == 1:
                rx = pl.ds(pl.multiple_of(t * rows, rows), rows)
                e = jnp.exp2(sx[rx, :] * c - top)
                total = jnp.concatenate([e, jnp.zeros_like(e)], axis=1)
                e = e.astype(jnp.bfloat16)
                px[rx, :] = e
                acc = dot(e, kx[:, :value], NN)
            else:
                total = jnp.zeros((rows, 128), jnp.float32)
                acc = jnp.zeros((rows, value), jnp.float32)

            def group(g, state):
                total, acc = state
                e = jnp.exp2(s[g, r, :] * c - top)
                total = total + (e[:, 0:128] + e[:, 128:256]) + (e[:, 256:384] + e[:, 384:512])
                e = e.astype(jnp.bfloat16)
                p[g, r, :] = e
                at = pl.ds(pl.multiple_of(g * keys, keys), keys)
                acc = acc + dot(e, ksel[b, at, :value], NN)
                return total, acc

            total, acc = lax.fori_loop(0, plane + 1, group, (total, acc))
            inv = 1.0 / jnp.sum(total, axis=1, keepdims=True)
            low = (acc * inv).astype(jnp.bfloat16)
            out[r, :] = low
            delta = jnp.sum(do[r, :].astype(jnp.float32) * low.astype(jnp.float32), axis=1, keepdims=True)
            scaled = (do[r, :].astype(jnp.float32) * inv).astype(jnp.bfloat16)
            dot_t[:, r] = scaled.T
            arow[r, :] = jnp.broadcast_to(inv * SCALE, (rows, 128))
            drow[r, :] = jnp.broadcast_to(inv * SCALE * delta, (rows, 128))
            return carry

        lax.fori_loop(0, tiles, tile, 0)

    lower = lax.broadcasted_iota(jnp.int32, (width, 128), 1) < BLOCK

    def plane_grad(g, carry):
        at = pl.ds(pl.multiple_of(g * keys, keys), keys)
        for b in range(2):
            every = slice(b * half, (b + 1) * half)
            acc[b, :value, :] = dot(dot_t[:, every], p[g, every, :], NN)

            def tile(t, carry, b=b):
                r = row_slice(b, t)
                dp = dot(do[r, :], ksel[b, at, :value], NT)
                e = p[g, r, :].astype(jnp.float32)
                p[g, r, :] = (e * (dp * arow[r, 0:1] - drow[r, 0:1])).astype(jnp.bfloat16)
                return carry

            lax.fori_loop(0, tiles, tile, 0)
            dk = dot(qt[:, every], p[g, every, :], NN)
            acc[b, :value, :] += dk[:value]
            acc[b, value:, :] = dk[value:]
        for m in range(PLANE // 2):
            j = g * PLANE + 2 * m
            even = jnp.zeros((width, 128), jnp.float32)
            odd = jnp.zeros((width, 128), jnp.float32)
            for b in range(2):
                pair = acc[b, :, m * 128:(m + 1) * 128]
                rolled = pltpu.roll(pair, 64, 1)
                w0 = wanted[b, j] == 1
                w1 = wanted[b, j + 1] == 1
                even = even + jnp.where(lower ^ w0, jnp.where(w0, rolled, pair), 0.0)
                odd = odd + jnp.where(lower ^ w1, jnp.where(w1, pair, rolled), 0.0)
            dlat[j] = even.astype(dlat.dtype)
            dlat[j + 1] = odd.astype(dlat.dtype)
        return carry

    def empty(j, carry):
        dlat[j] = jnp.zeros((width, 128), dlat.dtype)
        return carry

    lax.fori_loop((plane + 1) * PLANE, dlat.shape[0], empty, 0)
    accx[:value, :] = dot(dot_t[:, half:], px[...], NN)

    def tile_x(t, carry):
        r = row_slice(1, t)
        rx = pl.ds(pl.multiple_of(t * rows, rows), rows)
        dp = dot(do[r, :], kx[:, :value], NT)
        e = px[rx, :].astype(jnp.float32)
        px[rx, :] = (e * (dp * arow[r, 0:1] - drow[r, 0:1])).astype(jnp.bfloat16)
        return carry

    lax.fori_loop(0, tiles, tile_x, 0)
    dk = dot(qt[:, half:], px[...], NN)
    accx[:value, :] += dk[:value]
    accx[value:, :] = dk[value:]

    lax.fori_loop(0, plane + 1, plane_grad, 0)
    dlat[shard, :, :BLOCK] = (dlat[shard, :, :BLOCK].astype(jnp.float32) + accx[...]).astype(dlat.dtype)

    for b in range(2):
        def tile_q(t, carry, b=b):
            r = row_slice(b, t)
            if b == 1:
                rx = pl.ds(pl.multiple_of(t * rows, rows), rows)
                total = dot(px[rx, :], kx[...], NN)
            else:
                total = jnp.zeros((rows, width + pad), jnp.float32)

            def group(g, total):
                at = pl.ds(pl.multiple_of(g * keys, keys), keys)
                return total + dot(p[g, r, :], ksel[b, at, :], NN)

            total = lax.fori_loop(0, plane + 1, group, total)
            dq[r, :] = total[:, :width].astype(jnp.bfloat16)
            return carry

        lax.fori_loop(0, tiles, tile_q, 0)


def attention(shard, wanted, mask, q, do, latent, rows=256):
    n, width = q.shape
    value = do.shape[1]
    ranges = latent.shape[0] // 128
    vmem = pl.BlockSpec(memory_space=pltpu.VMEM)
    smem = pl.BlockSpec(memory_space=pltpu.SMEM)
    planes = ranges // PLANE
    return pl.pallas_call(
        functools.partial(attention_kernel, rows=rows),
        out_shape=(
            jax.ShapeDtypeStruct((n, value), jnp.bfloat16),
            jax.ShapeDtypeStruct((n, width), jnp.bfloat16),
            jax.ShapeDtypeStruct((ranges, width, 128), jnp.bfloat16),
        ),
        in_specs=[smem, smem, vmem, vmem, vmem, vmem],
        out_specs=(vmem, vmem, vmem),
        scratch_shapes=[
            pltpu.VMEM((n, width + 64), jnp.bfloat16),
            pltpu.VMEM((width, n), jnp.bfloat16),
            pltpu.VMEM((value, n), jnp.bfloat16),
            pltpu.VMEM((2, ranges * BLOCK, width + 64), jnp.bfloat16),
            pltpu.VMEM((BLOCK, width + 64), jnp.bfloat16),
            pltpu.VMEM((planes, n, PLANE * BLOCK), jnp.float32),
            pltpu.VMEM((planes, n, PLANE * BLOCK), jnp.bfloat16),
            pltpu.VMEM((n // 2, BLOCK), jnp.float32),
            pltpu.VMEM((n // 2, BLOCK), jnp.bfloat16),
            pltpu.VMEM((n, 128), jnp.float32),
            pltpu.VMEM((n, 128), jnp.float32),
            pltpu.VMEM((n, 128), jnp.float32),
            pltpu.VMEM((2, width, PLANE * BLOCK), jnp.float32),
            pltpu.VMEM((width, BLOCK), jnp.float32),
        ],
        compiler_params=pltpu.CompilerParams(vmem_limit_bytes=67043328),
    )(shard, wanted, mask, q, do, latent)


def tables(chosen, shard, shards):
    tok = chosen.shape[0]
    picked = jnp.any(chosen[:, :, None] == jnp.arange(2 * shards, dtype=jnp.int32)[None, None, :], axis=1)
    grouped = picked.reshape(tok, shards, 2)
    mine = jnp.arange(shards, dtype=jnp.int32) == shard
    per_range = jnp.any(grouped, axis=2) | mine[None, :]
    first = jnp.any(chosen == 2 * shard, axis=1)
    allowed = jnp.concatenate([per_range, first[:, None], jnp.ones((tok, 31), bool)], axis=1)
    mask = jnp.where(allowed, 0.0, -BIG).astype(jnp.bfloat16)
    second = jnp.any(picked.reshape(2, BLOCK, shards, 2)[..., 1], axis=1)
    wanted = jnp.where(mine[None, :], jnp.arange(2)[:, None] == 1, second).astype(jnp.int32)
    return mask, wanted


def body(queries, latent, cotangent, selection):
    tok, heads, width = queries.shape
    value = cotangent.shape[2]
    shards = lax.axis_size("ctx")
    shard = lax.axis_index("ctx").astype(jnp.int32)
    mask, wanted = tables(selection, shard, shards)
    everything = lax.all_gather(latent, "ctx", axis=0, tiled=True)
    out, dq, partial = attention(
        shard[None], wanted, mask, queries.reshape(tok * heads, width),
        cotangent.reshape(tok * heads, value), everything,
    )
    own = lax.psum_scatter(partial, "ctx", scatter_dimension=0, tiled=False)
    grad = lax.psum(own.astype(jnp.float32), "head").T
    return out.reshape(tok, heads, value), dq.reshape(tok, heads, width), grad


def solution(mesh):
    placed = (P("ctx", "head", None), P("ctx", None), P("ctx", "head", None), P("ctx", None))
    return jax.shard_map(
        body,
        mesh=mesh,
        in_specs=placed,
        out_specs=(P("ctx", "head", None), P("ctx", "head", None), P("ctx", None)),
        check_vma=False,
    )
```

profile of v0, /device:TPU:0, one launch (start us, length us, event | category | flops | bytes accessed | tf_op | source)
XLA Modules:
  0.0 280.1 jit_solution(8622559078072939325)
XLA Ops:
  7.2 0.0 all-gather.2.cloned.1.call-start
  7.2 1.7 copy.35
  8.9 0.0 all-gather.2.cloned.1.call-update
  8.9 0.0 reduce-scatter.2.cloned.1.call-start
  9.0 0.9 fusion
  9.9 0.1 reshape.36
  10.0 0.7 compare_reduce_fusion
  10.7 0.1 copy.33
  10.9 0.1 pad.2.clone
  10.9 0.1 reduce_or.38
  11.0 0.1 copy.31
  11.1 0.6 slice_reduce_fusion
  11.8 0.1 copy.30
  11.9 4.9 %copy.34 = bf16[128,16,576]{2,1,0:T(8,128)(2,1)} copy(bf16[128,16,576]{0,2,1:T(8,128)(2,1)} %param.4) | data formatting | bytes 4718592 | tf_op args[0]
  16.8 0.7 select_convert_fusion.1.wanted
  17.4 0.7 select_convert_fusion.mask
  18.2 42.5 %all-gather.2.cloned.1.call-done.latent = bf16[4096,576]{1,0:T(8,128)(2,1)} async-done(((bf16[128,576]{1,0:T(8,128)(2,1)}), bf16[4096,576]{1,0:T(8,128)(2,1)}) %all-gather.2.cloned.1.call-update) | async-done | bytes 4718608 | tf_op jit(solution)/shard_map/all_gather | solution.py:270
  60.7 35.3 %shard_map.67 = (bf16[2048,512]{1,0:T(8,128)(2,1)}, bf16[2048,576]{1,0:T(8,128)(2,1)}, bf16[32,576,128]{2,1,0:T(8,128)(2,1)}) custom-call(s32[1]{0:T(128)} %bitcast.me_ref, s32[2,32]{1,0:T(2,128)} %select_convert_fusion.1.wanted, bf16[128,64]{1,0:T(8,128)(2,1)} %select_convert_fusion.mask, bf16[2048,576]{1,0:T(8,128)(2,1)} %bitcast.15, ...), custom_call_target="tpu_custom_call" | custom-call | tf_op jit(solution)/shard_map/pallas_call | solution.py:221
  95.9 0.0 copy-start
  95.9 0.0 reduce-scatter.2.cloned.1.call-update
  95.9 0.0 all-reduce.2.cloned.1.call-start
  96.0 131.7 %reduce-scatter.2.cloned.1.call-done = bf16[1,576,128]{2,1,0:T(8,128)(2,1)} async-done(((bf16[32,576,128]{2,1,0:T(8,128)(2,1)}), bf16[1,576,128]{2,1,0:T(8,128)(2,1)}) %reduce-scatter.2.cloned.1.call-update) | async-done | bytes 147472 | tf_op jit(solution)/shard_map/reduce_scatter | solution.py:275
  227.7 1.6 convert_bitcast_fusion
  229.4 0.0 all-reduce.2.cloned.1.call-update
  229.4 0.0 copy-done
  229.4 3.1 %copy.36 = bf16[128,16,576]{0,2,1:T(8,128)(2,1)} copy(bf16[128,16,576]{2,1,0:T(8,128)(2,1)S(1)} %bitcast.16) | data formatting | bytes 4718592
  232.5 39.4 %all-reduce.2.cloned.1.call-done = f32[128,576]{0,1:T(8,128)} async-done(((f32[128,576]{0,1:T(8,128)}), f32[128,576]{0,1:T(8,128)}) %all-reduce.2.cloned.1.call-update) | async-done | bytes 294928 | tf_op jit(solution)/shard_map/psum | solution.py:276
  271.9 1.7 copy.38
  (5 shorter events, 0.0 us)
Async XLA Ops:
  7.2 53.5 %all-gather.2.cloned.1.call-start = ((), (), s32[]{:S(2)}) async-start(), calls=%async_computation.1 | async-start | bytes 5406720 | tf_op jit(solution)/shard_map/all_gather | solution.py:270
  8.9 218.8 %reduce-scatter.2.cloned.1.call-start = ((), (), s32[]{:S(2)}) async-start(), calls=%async_computation.2 | async-start | bytes 4866048 | tf_op jit(solution)/shard_map/reduce_scatter | solution.py:275
  95.9 133.5 %copy-start = (bf16[2048,576]{1,0:T(8,128)(2,1)S(1)}, bf16[2048,576]{1,0:T(8,128)(2,1)}, u32[]{:S(2)}) copy-start(bf16[2048,576]{1,0:T(8,128)(2,1)} %get-tuple-element.7) | copy-start | bytes 7077892
  95.9 175.9 %all-reduce.2.cloned.1.call-start = ((), (), s32[]{:S(2)}) async-start(), calls=%async_computation.3 | async-start | bytes 589824 | tf_op jit(solution)/shard_map/psum | solution.py:276
Sparse Core Ops, SparseCore 0:
  10.8 49.8 all-gather.1
  96.1 131.6 reduce-scatter.1
  230.6 41.1 all-reduce.1
where the time goes:
time: 280 us
  waiting for transfers between devices  214 us (76%)
  Pallas kernels  35.3 us (13%)
  between operations  13.8 us (5%)
  local copies, waits for them, and re-layouts  12 us (4%)
  other arithmetic  5.32 us (2%)
    reduce_scatter x1, waiting for transfers between devices, body(): own = lax.psum_scatter(partial, 'ctx', scatter_dimension=0, tiled=False)  132 us
    all_gather x1, waiting for transfers between devices, body(): everything = lax.all_gather(latent, 'ctx', axis=0, tiled=True)  42.5 us
    psum x1, waiting for transfers between devices, body(): grad = lax.psum(own.astype(jnp.float32), 'head').T  39.4 us
    pallas_call x1, Pallas kernels, attention(): pl.pallas_call(functools.partial(attention_kernel, rows=rows), out_shape=...  35.3 us
    unnamed x6, local copies, waits for them, and re-layouts  11.4 us
  transfers between devices with their start and end apart: 3, of which 3 were waited for; matrix products, arithmetic and copies ran while one was open for 4% of the time, Pallas kernels for 0%

commit v1 on v0

--- a/solution.py
+++ b/solution.py
@@ -261,19 +261,319 @@
     return mask, wanted
 
 
+MESH_ID = pl.DeviceIdType.MESH
+
+
+def ring(v, d):
+    return lax.rem(v + d + 4, 4)
+
+
+class Place:
+    def __init__(self):
+        idx = lax.axis_index("ctx").astype(jnp.int32)
+        self.idx = idx
+        self.z, self.x, self.c = idx // 8, lax.rem(idx // 2, 4), lax.rem(idx, 2)
+        self.y = lax.axis_index("head").astype(jnp.int32)
+
+    def at(self, dz=0, dx=0):
+        return (ring(self.z, dz) * 4 + ring(self.x, dx)) * 2 + self.c
+
+    def near(self, axis, d):
+        return {"ctx": self.at(d, 0) if axis == 0 else self.at(0, d)}
+
+    def twin(self):
+        return {"ctx": self.idx + 1 - 2 * self.c}
+
+
+def greet(targets):
+    barrier = pltpu.get_barrier_semaphore()
+    for t in targets:
+        pl.semaphore_signal(barrier, inc=1, device_id=t, device_id_type=MESH_ID)
+    pl.semaphore_wait(barrier, len(targets))
+
+
+class Wire:
+    def __init__(self, sems):
+        self.sems, self.sent = sems, []
+
+    def send(self, src, dst, recv, target):
+        copy = pltpu.make_async_remote_copy(
+            src_ref=src, dst_ref=dst, send_sem=self.sems.at[len(self.sent)], recv_sem=recv,
+            device_id=target, device_id_type=MESH_ID,
+        )
+        copy.start()
+        self.sent.append(copy)
+
+    def wait(self, dst, recv, target):
+        pltpu.make_async_remote_copy(
+            src_ref=dst, dst_ref=dst, send_sem=self.sems.at[0], recv_sem=recv,
+            device_id=target, device_id_type=MESH_ID,
+        ).wait_recv()
+
+    def finish(self):
+        for copy in self.sent:
+            copy.wait_send()
+
+
+class Gather:
+    def __init__(self, place, wire, full, recv, twin_recv):
+        self.place, self.wire, self.full, self.recv, self.twin_recv = place, wire, full, recv, twin_recv
+
+    def source(self, h, i, j):
+        return self.place.at(-i, -j) if h == 0 else self.place.at(-j, -i)
+
+    def rows(self, h, piece=None):
+        return pl.ds(h * 64, 64) if piece is None else pl.ds(h * 64 + piece * 32, 32)
+
+    def put(self, h, i, j, second, d, piece=None):
+        src = self.full.at[self.source(h, i, j), self.rows(h, piece)]
+        axis = (1 - h) if second else h
+        ni, nj = (i, (j + d) % 4) if second else ((i + d) % 4, j)
+        sem = self.recv.at[h, ni * 4 + nj, piece or 0]
+        self.wire.send(src, src, sem, self.place.near(axis, d))
+
+    def trade(self, h, i, j):
+        ref = self.full.at[self.source(h, i, j), self.rows(h)]
+        self.wire.send(ref, ref, self.twin_recv.at[h, i * 4 + j], self.place.twin())
+
+    def got(self, h, i, j):
+        src = self.source(h, i, j)
+        pieces = (0, 1) if (j == 2 or (j == 0 and i == 2)) else (None,)
+        for piece in pieces:
+            self.wire.wait(self.full.at[src, self.rows(h, piece)], self.recv.at[h, i * 4 + j, piece or 0], self.place.twin())
+
+    def both(self, h, i, j):
+        self.put(h, i, j, True, 1)
+        self.put(h, i, j, True, -1)
+
+    def start(self):
+        for h in range(2):
+            self.put(h, 0, 0, False, 1)
+            self.put(h, 0, 0, False, -1)
+        for h in range(2):
+            self.both(h, 0, 0)
+            self.trade(h, 0, 0)
+
+    def first(self):
+        for h in range(2):
+            for i, piece, d in ((1, 0, 1), (3, 1, -1)):
+                self.got(h, i, 0)
+                self.put(h, i, 0, False, d, piece)
+                self.both(h, i, 0)
+                self.trade(h, i, 0)
+
+    def relay(self, h, i):
+        for j, piece, d in ((1, 0, 1), (3, 1, -1)):
+            self.got(h, i, j)
+            self.put(h, i, j, True, d, piece)
+            self.trade(h, i, j)
+
+    def second(self):
+        for h in range(2):
+            self.relay(h, 0)
+        for h in range(2):
+            self.got(h, 2, 0)
+            self.both(h, 2, 0)
+            self.trade(h, 2, 0)
+
+    def third(self):
+        for i in (1, 3, 2):
+            for h in range(2):
+                self.relay(h, i)
+
+    def last(self):
+        for i in (0, 1, 3, 2):
+            for h in range(2):
+                self.got(h, i, 2)
+                self.trade(h, i, 2)
+
+    def traded(self):
+        for i in range(4):
+            for j in range(4):
+                for h in range(2):
+                    src = self.source(h, i, j) + 1 - 2 * self.place.c
+                    self.wire.wait(self.full.at[src, self.rows(h)], self.twin_recv.at[h, i * 4 + j], self.place.twin())
+
+
+def gather_kernel(own, full, sends, recv, twin_recv, local):
+    place = Place()
+    mine = pltpu.make_async_copy(own, full.at[place.idx], local)
+    mine.start()
+    greet([place.near(0, 1), place.near(0, -1), place.near(1, 1), place.near(1, -1), place.twin()])
+    mine.wait()
+    wire = Wire(sends)
+    g = Gather(place, wire, full, recv, twin_recv)
+    g.start()
+    g.first()
+    g.second()
+    g.third()
+    g.last()
+    g.traded()
+    wire.finish()
+
+
+def gather(latent, shards):
+    vmem = pl.BlockSpec(memory_space=pltpu.VMEM)
+    dma = pltpu.SemaphoreType.DMA
+    return pl.pallas_call(
+        gather_kernel,
+        out_shape=jax.ShapeDtypeStruct((shards,) + latent.shape, latent.dtype),
+        in_specs=[vmem],
+        out_specs=vmem,
+        scratch_shapes=[dma((72,)), dma((2, 16, 2)), dma((2, 16)), dma],
+        compiler_params=pltpu.CompilerParams(collective_id=0, has_side_effects=True),
+    )(latent)
+
+
+class Ring:
+    def __init__(self, place, wire, axis, block, halves, far, near, far_sem, near_sem):
+        self.place, self.wire, self.axis = place, wire, axis
+        self.block, self.halves = block, halves
+        self.far, self.near, self.far_sem, self.near_sem = far, near, far_sem, near_sem
+        me = place.z if axis == 0 else place.x
+        self.to = {d: ring(me, d) for d in (0, 1, 2, -1)}
+
+    def start(self):
+        for k, d in ((0, 1), (1, -1)):
+            self.wire.send(
+                self.block(self.to[2]).at[self.halves[k]], self.far.at[k], self.far_sem.at[k], self.place.near(self.axis, d)
+            )
+
+    def middle(self):
+        for k, d in ((0, 1), (1, -1)):
+            self.wire.wait(self.far.at[k], self.far_sem.at[k], self.place.near(self.axis, -d))
+            ref = self.block(self.to[d])
+            part = ref[self.halves[k]].astype(jnp.float32) + self.far[k].astype(jnp.float32)
+            ref[self.halves[k]] = part.astype(ref.dtype)
+            self.wire.send(ref, self.near.at[k], self.near_sem.at[k], self.place.near(self.axis, d))
+
+    def total(self):
+        for k, d in ((0, 1), (1, -1)):
+            self.wire.wait(self.near.at[k], self.near_sem.at[k], self.place.near(self.axis, -d))
+        mine = self.block(self.to[0])[...].astype(jnp.float32)
+        return mine + (self.near[0].astype(jnp.float32) + self.near[1].astype(jnp.float32))
+
+
+LOW = pl.ds(0, 288)
+HIGH = pl.ds(288, 288)
+PIECES = (pl.ds(0, 144), pl.ds(144, 144))
+
+
+def reduce_kernel(
+    part, out, twin_in, sum_a, sum_b, tot_a, tot_b, head_in, head_out, result,
+    far_ax, near_ax, far_az, near_az, far_bz, near_bz, far_bx, near_bx,
+    sends, twin_sem, sem_ax, sem_az, sem_bz, sem_bx, sem_y,
+):
+    place = Place()
+    z, x, c, y = place.z, place.x, place.c, place.y
+    others = [{"head": ring(y, d)} for d in (1, 2, 3)]
+    greet([place.near(0, 1), place.near(0, -1), place.near(1, 1), place.near(1, -1), place.twin()] + others)
+    wire = Wire(sends)
+    order = [ring(z, 2), ring(z, 1), ring(z, -1), z]
+    for n, g in enumerate(order):
+        wire.send(part.at[g, :, 1 - c], twin_in.at[g], twin_sem.at[g], place.twin())
+    b_ring = Ring(
+        place, wire, 0, lambda t: sum_b.at[t], (pl.ds(0, 2), pl.ds(2, 2)), far_bz, near_bz, sem_bz.at[0], sem_bz.at[1]
+    )
+    a_rings = []
+    for n, g in enumerate(order):
+        wire.wait(twin_in.at[g], twin_sem.at[g], place.twin())
+        for k in range(4):
+            both = part[g, k, c].astype(jnp.float32) + twin_in[g, k].astype(jnp.float32)
+            both = both.astype(part.dtype)
+            sum_a[g, k] = both[:288]
+            sum_b[g, k] = both[288:]
+        a_ring = Ring(
+            place, wire, 1, lambda t, g=g: sum_a.at[g, t], PIECES, far_ax.at[g], near_ax.at[g], sem_ax.at[g, 0], sem_ax.at[g, 1]
+        )
+        a_ring.start()
+        if n == 0:
+            b_ring.start()
+        if n == 2:
+            b_ring.middle()
+        if n > 0:
+            a_rings[n - 1].middle()
+        a_rings.append(a_ring)
+    a_rings[3].middle()
+    tot_b[...] = b_ring.total().astype(tot_b.dtype)
+    b_last = Ring(place, wire, 1, lambda t: tot_b.at[t], PIECES, far_bx, near_bx, sem_bx.at[0], sem_bx.at[1])
+    b_last.start()
+    a_last = Ring(place, wire, 0, lambda t: tot_a.at[t], PIECES, far_az, near_az, sem_az.at[0], sem_az.at[1])
+    for n, g in enumerate(order):
+        tot_a[g] = a_rings[n].total().astype(tot_a.dtype)
+        if n == 0:
+            a_last.start()
+        if n == 2:
+            a_last.middle()
+    b_last.middle()
+    low = a_last.total().astype(jnp.bfloat16)
+    high = b_last.total().astype(jnp.bfloat16)
+    for q in range(2):
+        head_out[q] = low[q * 144:(q + 1) * 144]
+        head_out[q + 2] = high[q * 144:(q + 1) * 144]
+    for d in (1, 2, 3):
+        t = ring(y, d)
+        wire.send(head_out.at[t], head_in.at[d - 1], sem_y.at[0, d - 1], others[d - 1])
+    for d in (1, 2, 3):
+        wire.wait(head_in.at[d - 1], sem_y.at[0, d - 1], others[d - 1])
+    mine = head_out[y].astype(jnp.float32) + head_in[0].astype(jnp.float32)
+    mine = mine + (head_in[1].astype(jnp.float32) + head_in[2].astype(jnp.float32))
+    result[y] = mine.astype(jnp.bfloat16)
+    for d in (1, 2, 3):
+        wire.send(result.at[y], result.at[y], sem_y.at[1, d - 1], others[d - 1])
+    for d in (1, 2, 3):
+        wire.wait(result.at[ring(y, -d)], sem_y.at[1, d - 1], others[d - 1])
+    for q in range(4):
+        out[q * 144:(q + 1) * 144, :] = result[q].astype(jnp.float32)
+    wire.finish()
+
+
+def reduce_all(part):
+    ranges, width, lanes = part.shape
+    vmem = pl.BlockSpec(memory_space=pltpu.VMEM)
+    dma = pltpu.SemaphoreType.DMA
+    low = jnp.bfloat16
+    half, piece = width // 2, width // 4
+    return pl.pallas_call(
+        reduce_kernel,
+        out_shape=jax.ShapeDtypeStruct((width, lanes), jnp.float32),
+        in_specs=[vmem],
+        out_specs=vmem,
+        scratch_shapes=[
+            pltpu.VMEM((4, 4, width, lanes), low),
+            pltpu.VMEM((4, 4, half, lanes), low),
+            pltpu.VMEM((4, 4, half, lanes), low),
+            pltpu.VMEM((4, half, lanes), low),
+            pltpu.VMEM((4, half, lanes), low),
+            pltpu.VMEM((3, piece, lanes), low),
+            pltpu.VMEM((4, piece, lanes), low),
+            pltpu.VMEM((4, piece, lanes), low),
+            pltpu.VMEM((4, 2, piece, lanes), low),
+            pltpu.VMEM((4, 2, half, lanes), low),
+            pltpu.VMEM((2, piece, lanes), low),
+            pltpu.VMEM((2, half, lanes), low),
+            pltpu.VMEM((2, 2, half, lanes), low),
+            pltpu.VMEM((2, 4, half, lanes), low),
+            pltpu.VMEM((2, piece, lanes), low),
+            pltpu.VMEM((2, half, lanes), low),
+            dma((40,)), dma((4,)), dma((4, 2, 2)), dma((2, 2)), dma((2, 2)), dma((2, 2)), dma((2, 3)),
+        ],
+        compiler_params=pltpu.CompilerParams(collective_id=1, has_side_effects=True, vmem_limit_bytes=32 << 20),
+    )(part.reshape(4, 4, 2, width, lanes))
+
+
 def body(queries, latent, cotangent, selection):
     tok, heads, width = queries.shape
     value = cotangent.shape[2]
     shards = lax.axis_size("ctx")
     shard = lax.axis_index("ctx").astype(jnp.int32)
     mask, wanted = tables(selection, shard, shards)
-    everything = lax.all_gather(latent, "ctx", axis=0, tiled=True)
+    everything = gather(latent, shards).reshape(shards * tok, width)
     out, dq, partial = attention(
         shard[None], wanted, mask, queries.reshape(tok * heads, width),
         cotangent.reshape(tok * heads, value), everything,
     )
-    own = lax.psum_scatter(partial, "ctx", scatter_dimension=0, tiled=False)
-    grad = lax.psum(own.astype(jnp.float32), "head").T
+    grad = reduce_all(partial).T
     return out.reshape(tok, heads, value), dq.reshape(tok, heads, width), grad
 
 

time: 280 us -> 171 us (0.61)
  waiting for transfers between devices: 214 us -> 0 us
  Pallas kernels: 35.3 us -> 151 us
  between operations: 13.8 us -> 0.69 us
  local copies, waits for them, and re-layouts: 12 us -> 14.9 us
    reduce_scatter x1 -> x0, waiting for transfers between devices: 132 us -> none  [body(): own = lax.psum_scatter(partial, 'ctx', scatter_dimension=0, tiled=False)]
    pallas_call x0 -> x2, Pallas kernels: none -> 116 us  [the longest x1 86.4 us: reduce_all(): pl.pallas_call(reduce_kernel, out_shape=jax.ShapeDtypeStruct((width, lane...]
    all_gather x1 -> x0, waiting for transfers between devices: 42.5 us -> none  [body(): everything = lax.all_gather(latent, 'ctx', axis=0, tiled=True)]
    psum x1 -> x0, waiting for transfers between devices: 39.4 us -> none  [body(): grad = lax.psum(own.astype(jnp.float32), 'head').T]
    unnamed x6, local copies, waits for them, and re-layouts: 11.4 us -> 14.3 us
  transfers between devices with their start and end apart: 3 -> 0, of which waited for: 3 -> 0; matrix products, arithmetic and copies ran while one was open for 4% -> 0% of each run, Pallas kernels for 0% -> 0%
where the time goes in v1:
time: 171 us; the launch traced here: 170 us
  Pallas kernels  151 us (88%)
  local copies, waits for them, and re-layouts  14.9 us (9%)
  other arithmetic  3.68 us (2%)
    pallas_call x1, Pallas kernels, reduce_all(): pl.pallas_call(reduce_kernel, out_shape=jax.ShapeDtypeStruct((width, lane...  86.4 us
    pallas_call x1, Pallas kernels, attention(): pl.pallas_call(functools.partial(attention_kernel, rows=rows), out_shape=...  35.5 us
    pallas_call x1, Pallas kernels, gather(): pl.pallas_call(gather_kernel, out_shape=jax.ShapeDtypeStruct((shards,) +...  29.2 us
    unnamed x6, local copies, waits for them, and re-layouts  14.3 us

profile of v1, /device:TPU:0, one launch (start us, length us, event | category | flops | bytes accessed | tf_op | source)
XLA Modules:
  0.0 170.2 jit_solution(9063470528867002982)
XLA Ops:
  0.6 0.7 compare_reduce_fusion
  1.4 0.1 pad.2.clone
  1.5 0.9 fusion
  2.3 0.1 copy.33
  2.5 0.1 reduce_or.38
  2.5 0.1 copy.31
  2.7 0.7 select_convert_fusion.mask
  3.4 0.1 reshape.40
  3.5 0.6 slice_reduce_fusion
  4.1 0.1 copy.30
  4.2 0.7 select_convert_fusion.1.wanted
  4.9 1.7 %copy.35.own = bf16[128,576]{1,0:T(8,128)(2,1)} copy(bf16[128,576]{0,1:T(8,128)(2,1)} %param.5) | data formatting | bytes 294912 | tf_op args[1]
  6.6 4.9 %copy.34 = bf16[128,16,576]{2,1,0:T(8,128)(2,1)} copy(bf16[128,16,576]{0,2,1:T(8,128)(2,1)} %param.4) | data formatting | bytes 4718592 | tf_op args[0]
  11.5 29.2 %shard_map.67 = bf16[32,128,576]{2,1,0:T(8,128)(2,1)} custom-call(bf16[128,576]{1,0:T(8,128)(2,1)} %copy.35.own), custom_call_target="tpu_custom_call" | custom-call | tf_op jit(solution)/shard_map/pallas_call | solution.py:418
  40.7 35.5 %shard_map.68 = (bf16[2048,512]{1,0:T(8,128)(2,1)}, bf16[2048,576]{1,0:T(8,128)(2,1)}, bf16[32,576,128]{2,1,0:T(8,128)(2,1)}) custom-call(s32[1]{0:T(128)} %bitcast.me_ref, s32[2,32]{1,0:T(2,128)} %select_convert_fusion.1.wanted, bf16[128,64]{1,0:T(8,128)(2,1)} %select_convert_fusion.mask, bf16[2048,576]{1,0:T(8,128)(2,1)} %bitcast.16, ...), custom_call_target="tpu_custom_call" | custom-call | tf_op jit(solution)/shard_map/pallas_call | solution.py:221
  76.1 4.7 %copy.36 = bf16[128,16,576]{0,2,1:T(8,128)(2,1)} copy(bf16[128,16,576]{2,1,0:T(8,128)(2,1)} %bitcast.17) | data formatting | bytes 4718592
  80.8 0.0 copy-start
  80.8 2.3 %copy-done = bf16[32,576,128]{2,1,0:T(8,128)(2,1)S(1)} copy-done((bf16[32,576,128]{2,1,0:T(8,128)(2,1)S(1)}, bf16[32,576,128]{2,1,0:T(8,128)(2,1)}, u32[]{:S(2)}) %copy-start) | copy-done | bytes 4718616
  83.1 86.4 %shard_map.69 = f32[576,128]{1,0:T(8,128)S(1)} custom-call(bf16[4,4,2,576,128]{4,3,2,1,0:T(8,128)(2,1)S(1)} %bitcast.13), custom_call_target="tpu_custom_call" | custom-call | tf_op jit(solution)/shard_map/pallas_call | solution.py:537
  169.5 0.7 copy.38
  (5 shorter events, 0.0 us)
Async XLA Ops:
  80.8 2.3 %copy-start = (bf16[32,576,128]{2,1,0:T(8,128)(2,1)S(1)}, bf16[32,576,128]{2,1,0:T(8,128)(2,1)}, u32[]{:S(2)}) copy-start(bf16[32,576,128]{2,1,0:T(8,128)(2,1)} %get-tuple-element.8) | copy-start | bytes 14155780

commit v2 on v1

--- a/solution.py
+++ b/solution.py
@@ -12,6 +12,9 @@
 LOG2E = 1.4426950408889634
 BIG = 1e30
 PLANE = 8
+KEYS = PLANE * BLOCK
+HEADS = 16
+HALF = HEADS * BLOCK
 NT = (((1,), (1,)), ((), ()))
 NN = (((1,), (0,)), ((), ()))
 
@@ -20,229 +23,326 @@
     return lax.dot_general(a, b, dims, preferred_element_type=jnp.float32)
 
 
-def attention_kernel(
-    me_ref, wanted, mask, q, do, latent, out, dq, dlat,
-    qx, qt, dot_t, ksel, kx, s, p, sx, px, mrow, arow, drow, acc, accx, *, rows,
-):
+def swap(x):
+    return pltpu.roll(x, 64, 1)
+
+
+class Attention:
+    def __init__(self, shard, wanted, width, value, refs):
+        self.shard, self.wanted, self.width, self.value = shard, wanted, width, value
+        (self.qx, self.qt, self.do, self.dot_t, self.ksel, self.kx, self.s, self.p, self.sx, self.px,
+         self.mrow, self.arow, self.drow, self.wide, self.accx) = refs
+        self.pad = self.qx.shape[1] - width
+
+    def keys(self, g):
+        return pl.ds(pl.multiple_of(g * KEYS, KEYS), KEYS)
+
+    def block(self, b):
+        return slice(b * HALF, (b + 1) * HALF)
+
+    def load_queries(self, q, mask):
+        width = self.width
+        lower = lax.broadcasted_iota(jnp.int32, (width, 128), 1) < BLOCK
+
+        def pair(m, carry):
+            q0 = q[2 * m].astype(jnp.float32)
+            q1 = q[2 * m + 1].astype(jnp.float32)
+            for b in range(2):
+                x = jnp.where(lower, q0, swap(q1)) if b == 0 else jnp.where(lower, swap(q0), q1)
+                x = x.astype(jnp.bfloat16)
+                at = pl.ds(pl.multiple_of(b * HALF + m * 128, 128), 128)
+                self.qt[:, at] = x
+                self.qx[at, :width] = x.T
+                bias = mask[b * BLOCK:(b + 1) * BLOCK, :]
+                self.qx[at, width:] = jnp.concatenate([bias, bias], axis=0)
+            return carry
+
+        lax.fori_loop(0, HEADS // 2, pair, 0)
+
+    def load_cotangent(self, do):
+        for b in range(2):
+            for pair in range(self.value // 256):
+                for k in range(2):
+                    lanes = slice((2 * pair + k) * 128, (2 * pair + k + 1) * 128)
+                    self.mrow[self.block(k), :] = do[self.block(b), lanes].astype(jnp.float32)
+
+                def head(h, carry, b=b, pair=pair):
+                    at = pl.ds(pl.multiple_of(b * HALF + h * BLOCK, BLOCK), BLOCK)
+                    for k in range(2):
+                        rows = self.mrow[pl.ds(k * HALF + h, BLOCK, stride=HEADS), :]
+                        lanes = slice((2 * pair + k) * 128, (2 * pair + k + 1) * 128)
+                        self.do[at, lanes] = rows.astype(jnp.bfloat16)
+                    return carry
+
+                lax.fori_loop(0, HEADS, head, 0)
+
+    def pick(self, latent, g):
+        width = self.width
+        lower = lax.broadcasted_iota(jnp.int32, (width, 128), 1) < BLOCK
+        column = lax.broadcasted_iota(jnp.int32, (128, self.pad), 1)
+        slot = lax.broadcasted_iota(jnp.int32, (128, self.pad), 0) // BLOCK
+
+        def pair(m, carry):
+            j = g * PLANE + 2 * m
+            k0 = latent[j].astype(jnp.float32)
+            k1 = latent[j + 1].astype(jnp.float32)
+            r0, r1 = swap(k0), swap(k1)
+            at = pl.ds(pl.multiple_of(j * BLOCK, 128), 128)
+            for b in range(2):
+                w0, w1 = self.wanted[b, j] == 1, self.wanted[b, j + 1] == 1
+                x = jnp.where(lower, jnp.where(w0, r0, k0), jnp.where(w1, k1, r1)).astype(jnp.bfloat16)
+                self.ksel[b, at, :width] = x.T
+                self.ksel[b, at, width:] = jnp.where(column == j + slot, 1.0, 0.0).astype(jnp.bfloat16)
+            return carry
+
+        lax.fori_loop(0, PLANE // 2, pair, 0)
+
+    def pick_own(self, own):
+        self.kx[:, :self.width] = own.T[:BLOCK, :]
+        column = lax.broadcasted_iota(jnp.int32, (BLOCK, self.pad), 1)
+        self.kx[:, self.width:] = jnp.where(column == 32, 1.0, 0.0).astype(jnp.bfloat16)
+
+    def scores(self, g, b, own):
+        r = self.block(b)
+        x = dot(self.qx[r, :], self.ksel[b, self.keys(g), :], NT)
+        if own:
+            lane = lax.broadcasted_iota(jnp.int32, (HALF, KEYS), 1)
+            row = lax.broadcasted_iota(jnp.int32, (HALF, KEYS), 0)
+            late = (lane // BLOCK == lax.rem(self.shard, PLANE)) & (lane % BLOCK > row % BLOCK)
+            x = jnp.where(late, -BIG, x)
+        self.s[g] = x
+        top = jnp.maximum(self.s[g, :, 0:128], self.s[g, :, 128:256])
+        for k in range(2, KEYS // 128):
+            top = jnp.maximum(top, self.s[g, :, k * 128:(k + 1) * 128])
+        if own:
+            if b == 1:
+                y = dot(self.qx[r, :], self.kx[...], NT)
+                self.sx[...] = y
+                top = jnp.maximum(top, jnp.concatenate([y, y], axis=1))
+            self.mrow[r, :] = top
+        else:
+            self.mrow[r, :] = jnp.maximum(self.mrow[r, :], top)
+
+    def softmax_start(self, b):
+        c = SCALE * LOG2E
+        r = self.block(b)
+        top = jnp.max(self.mrow[r, :], axis=1, keepdims=True) * c
+        self.mrow[r, :] = jnp.broadcast_to(top, (HALF, 128))
+        if b == 0:
+            self.wide[r, :] = jnp.zeros((HALF, self.value), jnp.float32)
+            self.arow[r, :] = jnp.zeros((HALF, 128), jnp.float32)
+        else:
+            e = jnp.exp2(self.sx[...] * c - top)
+            self.arow[r, :] = jnp.concatenate([e, jnp.zeros_like(e)], axis=1)
+            self.px[...] = e.astype(jnp.bfloat16)
+            self.wide[r, :] = dot(self.px[...], self.kx[:, :self.value], NN)
+
+    def softmax(self, g, b):
+        c = SCALE * LOG2E
+        r = self.block(b)
+        total = self.arow[r, :]
+        for k in range(KEYS // 128):
+            lanes = slice(k * 128, (k + 1) * 128)
+            e = jnp.exp2(self.s[g, :, lanes] * c - self.mrow[r, :])
+            total = total + e
+            self.p[g, r, lanes] = e.astype(jnp.bfloat16)
+        self.arow[r, :] = total
+        self.wide[r, :] += dot(self.p[g, r, :], self.ksel[b, self.keys(g), :self.value], NN)
+
+    def softmax_end(self, b, out):
+        def tile(t, carry):
+            r = pl.ds(pl.multiple_of(b * HALF + t * 256, 256), 256)
+            inv = 1.0 / jnp.sum(self.arow[r, :], axis=1, keepdims=True)
+            full = self.wide[r, :] * inv
+            self.wide[r, :] = full
+            do = self.do[r, :].astype(jnp.float32)
+            delta = jnp.sum(do * full.astype(jnp.bfloat16).astype(jnp.float32), axis=1, keepdims=True)
+            self.dot_t[:, r] = (do * inv).astype(jnp.bfloat16).T
+            self.arow[r, :] = jnp.broadcast_to(inv * SCALE, (256, 128))
+            self.drow[r, :] = jnp.broadcast_to(inv * SCALE * delta, (256, 128))
+            return carry
+
+        lax.fori_loop(0, HALF // 256, tile, 0)
+        for k in range(self.value // 128):
+            lanes = slice(k * 128, (k + 1) * 128)
+            self.mrow[self.block(b), :] = self.wide[self.block(b), lanes]
+
+            def token(t, carry, lanes=lanes):
+                at = pl.ds(pl.multiple_of((b * BLOCK + t) * HEADS, HEADS), HEADS)
+                out[at, lanes] = self.mrow[pl.ds(b * HALF + t, HEADS, stride=BLOCK), :].astype(jnp.bfloat16)
+                return carry
+
+            lax.fori_loop(0, BLOCK, token, 0, unroll=8)
+
+    def acc(self, b, at):
+        return self.s.at[2 + b, at]
+
+    def grads(self, g):
+        value, width = self.value, self.width
+        for b in range(2):
+            r = self.block(b)
+            top, rest = self.acc(b, slice(0, value)), self.acc(b, slice(value, width))
+            top[...] = dot(self.dot_t[:, r], self.p[g, r, :], NN)
+            self.s[b] = dot(self.do[r, :], self.ksel[b, self.keys(g), :value], NT)
+            for k in range(KEYS // 128):
+                lanes = slice(k * 128, (k + 1) * 128)
+                e = self.p[g, r, lanes].astype(jnp.float32)
+                d = e * (self.s[b, :, lanes] * self.arow[r, :] - self.drow[r, :])
+                self.p[g, r, lanes] = d.astype(jnp.bfloat16)
+            dk = dot(self.qt[:, r], self.p[g, r, :], NN)
+            top[...] += dk[:value]
+            rest[...] = dk[value:]
+
+    def grads_extra(self):
+        value, r = self.value, self.block(1)
+        self.accx[:value, :] = dot(self.dot_t[:, r], self.px[...], NN)
+        dp = dot(self.do[r, :], self.kx[:, :value], NT)
+        e = self.px[...].astype(jnp.float32)
+        self.px[...] = (e * (dp * self.arow[r, 0:BLOCK] - self.drow[r, 0:BLOCK])).astype(jnp.bfloat16)
+        dk = dot(self.qt[:, r], self.px[...], NN)
+        self.accx[:value, :] += dk[:value]
+        self.accx[value:, :] = dk[value:]
+
+    def spread(self, g, m):
+        lower = lax.broadcasted_iota(jnp.int32, (self.width, 128), 1) < BLOCK
+        j = g * PLANE + 2 * m
+        even = jnp.zeros((self.width, 128), jnp.float32)
+        odd = jnp.zeros((self.width, 128), jnp.float32)
+        for b in range(2):
+            x = self.acc(b, slice(0, self.width))[:, m * 128:(m + 1) * 128]
+            rolled = swap(x)
+            w0 = self.wanted[b, j] == 1
+            w1 = self.wanted[b, j + 1] == 1
+            even = even + jnp.where(lower ^ w0, jnp.where(w0, rolled, x), 0.0)
+            odd = odd + jnp.where(lower ^ w1, jnp.where(w1, x, rolled), 0.0)
+        return even, odd
+
+    def wide_at(self, b, n):
+        at = (2 * b + n) * self.width
+        return pl.ds(at, self.width)
+
+    def grad_queries_start(self):
+        for n in range(2):
+            self.wide[self.wide_at(0, n), :] = jnp.zeros((self.width, HALF // 2), jnp.float32)
+            rows = self.px[n * HALF // 2:(n + 1) * HALF // 2, :]
+            self.wide[self.wide_at(1, n), :] = dot(self.kx[:, :self.width].T, rows, NT)
+
+    def grad_queries(self, g):
+        for b in range(2):
+            kt = self.ksel[b, self.keys(g), :self.width].T
+            for n in range(2):
+                rows = self.p[g, b * HALF + n * HALF // 2:b * HALF + (n + 1) * HALF // 2, :]
+                self.wide[self.wide_at(b, n), :] += dot(kt, rows, NT)
+
+    def grad_queries_end(self, dq):
+        lower = lax.broadcasted_iota(jnp.int32, (self.width, 128), 1) < BLOCK
+        for m in range(HEADS // 2):
+            n, lanes = m // 4, slice((m % 4) * 128, (m % 4 + 1) * 128)
+            y0 = self.wide[self.wide_at(0, n), lanes]
+            y1 = self.wide[self.wide_at(1, n), lanes]
+            dq[2 * m] = jnp.where(lower, y0, swap(y1)).astype(jnp.bfloat16)
+            dq[2 * m + 1] = jnp.where(lower, swap(y0), y1).astype(jnp.bfloat16)
+
+
+def scratch(width, value, ranges):
+    n, low, f32 = 2 * HALF, jnp.bfloat16, jnp.float32
+    planes = ranges // PLANE
+    return [
+        pltpu.VMEM((n, width + 64), low),
+        pltpu.VMEM((width, n), low),
+        pltpu.VMEM((n, value), low),
+        pltpu.VMEM((value, n), low),
+        pltpu.VMEM((2, ranges * BLOCK, width + 64), low),
+        pltpu.VMEM((BLOCK, width + 64), low),
+        pltpu.VMEM((planes, HALF, KEYS), f32),
+        pltpu.VMEM((planes, n, KEYS), low),
+        pltpu.VMEM((HALF, BLOCK), f32),
+        pltpu.VMEM((HALF, BLOCK), low),
+        pltpu.VMEM((n, 128), f32),
+        pltpu.VMEM((n, 128), f32),
+        pltpu.VMEM((n, 128), f32),
+        pltpu.VMEM((4 * width, HALF // 2), f32),
+        pltpu.VMEM((width, BLOCK), f32),
+    ]
+
+
+def attention_kernel(me_ref, wanted, mask, q_in, do_in, latent, out_hbm, dq_hbm, dlat, q, do, sems, *refs):
     shard = me_ref[0]
     plane = shard // PLANE
     width = q.shape[1]
-    value = do.shape[1]
-    half = BLOCK * 16
-    keys = PLANE * BLOCK
-    pad = qx.shape[1] - width
-    c = SCALE * LOG2E
-
-    column = lax.broadcasted_iota(jnp.int32, (BLOCK, pad), 1)
-
-    def pick(j, carry):
-        one = jnp.where(column == j, 1.0, 0.0).astype(jnp.bfloat16)
-        k0 = latent[pl.ds(pl.multiple_of(j * 128, 128), 64), :]
-        k1 = latent[pl.ds(pl.multiple_of(j * 128 + 64, 64), 64), :]
-        at = pl.ds(pl.multiple_of(j * 64, 64), 64)
-        for b in range(2):
-            ksel[b, at, :width] = jnp.where(wanted[b, j] == 1, k1, k0)
-            ksel[b, at, width:] = one
-        return carry
-
-    lax.fori_loop(0, (plane + 1) * PLANE, pick, 0)
-    kx[:, :width] = latent[pl.ds(pl.multiple_of(shard * 128, 128), 64), :]
-    kx[:, width:] = jnp.where(column == 32, 1.0, 0.0).astype(jnp.bfloat16)
-
-    qx[:, :width] = q[...]
-    qx[:, width:] = jnp.broadcast_to(mask[...][:, None, :], (128, 16, pad)).reshape(2048, pad)
-    qt[...] = q[...].T
-
-    lane = lax.broadcasted_iota(jnp.int32, (rows, keys), 1)
-    row = lax.broadcasted_iota(jnp.int32, (rows, keys), 0)
-    tiles = half // rows
-
-    def row_slice(b, t):
-        return pl.ds(pl.multiple_of(b * half + t * rows, rows), rows)
-
-    def scores(g, b, own):
-        at = pl.ds(pl.multiple_of(g * keys, keys), keys)
-
-        def tile(t, carry):
-            r = row_slice(b, t)
-            x = dot(qx[r, :], ksel[b, at, :], NT)
-            if own:
-                slot = lax.rem(shard, PLANE)
-                late = (lane // BLOCK == slot) & (lane % BLOCK > (row + t * rows) // 16)
-                x = jnp.where(late, -BIG, x)
-            s[g, r, :] = x
-            top = jnp.maximum(
-                jnp.maximum(x[:, 0:128], x[:, 128:256]), jnp.maximum(x[:, 256:384], x[:, 384:512])
-            )
-            if own:
-                if b == 1:
-                    y = dot(qx[r, :], kx[...], NT)
-                    sx[pl.ds(pl.multiple_of(t * rows, rows), rows), :] = y
-                    top = jnp.maximum(top, jnp.concatenate([y, y], axis=1))
-                mrow[r, :] = top
-            else:
-                mrow[r, :] = jnp.maximum(mrow[r, :], top)
+    out, dq = do, q
+    a = Attention(shard, wanted, width, do.shape[1], refs)
+    get_q = pltpu.make_async_copy(q_in, q, sems.at[0])
+    get_do = pltpu.make_async_copy(do_in, do, sems.at[1])
+    put_out = pltpu.make_async_copy(out, out_hbm, sems.at[2])
+    put_dq = pltpu.make_async_copy(dq, dq_hbm, sems.at[3])
+    get_q.start()
+    get_do.start()
+    get_q.wait()
+    get_do.wait()
+
+    def each(count, step):
+        def body(g, carry):
+            step(g)
             return carry
 
-        lax.fori_loop(0, tiles, tile, 0)
-
-    scores(plane, 0, True)
-    scores(plane, 1, True)
-
-    def score_step(g, carry):
-        scores(g, 0, False)
-        scores(g, 1, False)
-        return carry
-
-    lax.fori_loop(0, plane, score_step, 0)
-
+        lax.fori_loop(0, count, body, 0)
+
+    a.load_queries(q, mask)
+    a.load_cotangent(do)
+    each(plane + 1, lambda g: a.pick(latent, g))
+    a.pick_own(latent[shard])
     for b in range(2):
-        def tile(t, carry, b=b):
-            r = row_slice(b, t)
-            top = jnp.max(mrow[r, :], axis=1, keepdims=True) * c
-            if b == 1:
-                rx = pl.ds(pl.multiple_of(t * rows, rows), rows)
-                e = jnp.exp2(sx[rx, :] * c - top)
-                total = jnp.concatenate([e, jnp.zeros_like(e)], axis=1)
-                e = e.astype(jnp.bfloat16)
-                px[rx, :] = e
-                acc = dot(e, kx[:, :value], NN)
-            else:
-                total = jnp.zeros((rows, 128), jnp.float32)
-                acc = jnp.zeros((rows, value), jnp.float32)
-
-            def group(g, state):
-                total, acc = state
-                e = jnp.exp2(s[g, r, :] * c - top)
-                total = total + (e[:, 0:128] + e[:, 128:256]) + (e[:, 256:384] + e[:, 384:512])
-                e = e.astype(jnp.bfloat16)
-                p[g, r, :] = e
-                at = pl.ds(pl.multiple_of(g * keys, keys), keys)
-                acc = acc + dot(e, ksel[b, at, :value], NN)
-                return total, acc
-
-            total, acc = lax.fori_loop(0, plane + 1, group, (total, acc))
-            inv = 1.0 / jnp.sum(total, axis=1, keepdims=True)
-            low = (acc * inv).astype(jnp.bfloat16)
-            out[r, :] = low
-            delta = jnp.sum(do[r, :].astype(jnp.float32) * low.astype(jnp.float32), axis=1, keepdims=True)
-            scaled = (do[r, :].astype(jnp.float32) * inv).astype(jnp.bfloat16)
-            dot_t[:, r] = scaled.T
-            arow[r, :] = jnp.broadcast_to(inv * SCALE, (rows, 128))
-            drow[r, :] = jnp.broadcast_to(inv * SCALE * delta, (rows, 128))
-            return carry
-
-        lax.fori_loop(0, tiles, tile, 0)
-
-    lower = lax.broadcasted_iota(jnp.int32, (width, 128), 1) < BLOCK
-
-    def plane_grad(g, carry):
-        at = pl.ds(pl.multiple_of(g * keys, keys), keys)
-        for b in range(2):
-            every = slice(b * half, (b + 1) * half)
-            acc[b, :value, :] = dot(dot_t[:, every], p[g, every, :], NN)
-
-            def tile(t, carry, b=b):
-                r = row_slice(b, t)
-                dp = dot(do[r, :], ksel[b, at, :value], NT)
-                e = p[g, r, :].astype(jnp.float32)
-                p[g, r, :] = (e * (dp * arow[r, 0:1] - drow[r, 0:1])).astype(jnp.bfloat16)
-                return carry
-
-            lax.fori_loop(0, tiles, tile, 0)
-            dk = dot(qt[:, every], p[g, every, :], NN)
-            acc[b, :value, :] += dk[:value]
-            acc[b, value:, :] = dk[value:]
+        a.scores(plane, b, True)
+        each(plane, lambda g, b=b: a.scores(g, b, False))
+        a.softmax_start(b)
+        each(plane + 1, lambda g, b=b: a.softmax(g, b))
+        a.softmax_end(b, out)
+    put_out.start()
+    a.grads_extra()
+
+    def grads(g):
+        a.grads(g)
         for m in range(PLANE // 2):
+            even, odd = a.spread(g, m)
             j = g * PLANE + 2 * m
-            even = jnp.zeros((width, 128), jnp.float32)
-            odd = jnp.zeros((width, 128), jnp.float32)
-            for b in range(2):
-                pair = acc[b, :, m * 128:(m + 1) * 128]
-                rolled = pltpu.roll(pair, 64, 1)
-                w0 = wanted[b, j] == 1
-                w1 = wanted[b, j + 1] == 1
-                even = even + jnp.where(lower ^ w0, jnp.where(w0, rolled, pair), 0.0)
-                odd = odd + jnp.where(lower ^ w1, jnp.where(w1, pair, rolled), 0.0)
             dlat[j] = even.astype(dlat.dtype)
             dlat[j + 1] = odd.astype(dlat.dtype)
+
+    def empty(j, carry):
+        dlat[j] = jnp.zeros(dlat.shape[1:], dlat.dtype)
         return carry
 
-    def empty(j, carry):
-        dlat[j] = jnp.zeros((width, 128), dlat.dtype)
-        return carry
-
+    each(plane + 1, grads)
     lax.fori_loop((plane + 1) * PLANE, dlat.shape[0], empty, 0)
-    accx[:value, :] = dot(dot_t[:, half:], px[...], NN)
-
-    def tile_x(t, carry):
-        r = row_slice(1, t)
-        rx = pl.ds(pl.multiple_of(t * rows, rows), rows)
-        dp = dot(do[r, :], kx[:, :value], NT)
-        e = px[rx, :].astype(jnp.float32)
-        px[rx, :] = (e * (dp * arow[r, 0:1] - drow[r, 0:1])).astype(jnp.bfloat16)
-        return carry
-
-    lax.fori_loop(0, tiles, tile_x, 0)
-    dk = dot(qt[:, half:], px[...], NN)
-    accx[:value, :] += dk[:value]
-    accx[value:, :] = dk[value:]
-
-    lax.fori_loop(0, plane + 1, plane_grad, 0)
-    dlat[shard, :, :BLOCK] = (dlat[shard, :, :BLOCK].astype(jnp.float32) + accx[...]).astype(dlat.dtype)
-
-    for b in range(2):
-        def tile_q(t, carry, b=b):
-            r = row_slice(b, t)
-            if b == 1:
-                rx = pl.ds(pl.multiple_of(t * rows, rows), rows)
-                total = dot(px[rx, :], kx[...], NN)
-            else:
-                total = jnp.zeros((rows, width + pad), jnp.float32)
-
-            def group(g, total):
-                at = pl.ds(pl.multiple_of(g * keys, keys), keys)
-                return total + dot(p[g, r, :], ksel[b, at, :], NN)
-
-            total = lax.fori_loop(0, plane + 1, group, total)
-            dq[r, :] = total[:, :width].astype(jnp.bfloat16)
-            return carry
-
-        lax.fori_loop(0, tiles, tile_q, 0)
-
-
-def attention(shard, wanted, mask, q, do, latent, rows=256):
-    n, width = q.shape
+    dlat[shard, :, :BLOCK] = (dlat[shard, :, :BLOCK].astype(jnp.float32) + a.accx[...]).astype(dlat.dtype)
+    a.grad_queries_start()
+    each(plane + 1, a.grad_queries)
+    a.grad_queries_end(dq)
+    put_dq.start()
+    put_dq.wait()
+    put_out.wait()
+
+
+def attention(shard, wanted, mask, q, do, latent):
+    heads, width, tok = q.shape
     value = do.shape[1]
-    ranges = latent.shape[0] // 128
+    ranges = latent.shape[0]
     vmem = pl.BlockSpec(memory_space=pltpu.VMEM)
     smem = pl.BlockSpec(memory_space=pltpu.SMEM)
-    planes = ranges // PLANE
+    hbm = pl.BlockSpec(memory_space=pl.ANY)
     return pl.pallas_call(
-        functools.partial(attention_kernel, rows=rows),
+        attention_kernel,
         out_shape=(
-            jax.ShapeDtypeStruct((n, value), jnp.bfloat16),
-            jax.ShapeDtypeStruct((n, width), jnp.bfloat16),
-            jax.ShapeDtypeStruct((ranges, width, 128), jnp.bfloat16),
+            jax.ShapeDtypeStruct((heads * tok, value), jnp.bfloat16),
+            jax.ShapeDtypeStruct((heads, width, tok), jnp.bfloat16),
+            jax.ShapeDtypeStruct((ranges, width, tok), jnp.bfloat16),
         ),
-        in_specs=[smem, smem, vmem, vmem, vmem, vmem],
-        out_specs=(vmem, vmem, vmem),
+        in_specs=[smem, smem, vmem, hbm, hbm, vmem],
+        out_specs=(hbm, hbm, vmem),
         scratch_shapes=[
-            pltpu.VMEM((n, width + 64), jnp.bfloat16),
-            pltpu.VMEM((width, n), jnp.bfloat16),
-            pltpu.VMEM((value, n), jnp.bfloat16),
-            pltpu.VMEM((2, ranges * BLOCK, width + 64), jnp.bfloat16),
-            pltpu.VMEM((BLOCK, width + 64), jnp.bfloat16),
-            pltpu.VMEM((planes, n, PLANE * BLOCK), jnp.float32),
-            pltpu.VMEM((planes, n, PLANE * BLOCK), jnp.bfloat16),
-            pltpu.VMEM((n // 2, BLOCK), jnp.float32),
-            pltpu.VMEM((n // 2, BLOCK), jnp.bfloat16),
-            pltpu.VMEM((n, 128), jnp.float32),
-            pltpu.VMEM((n, 128), jnp.float32),
-            pltpu.VMEM((n, 128), jnp.float32),
-            pltpu.VMEM((2, width, PLANE * BLOCK), jnp.float32),
-            pltpu.VMEM((width, BLOCK), jnp.float32),
-        ],
+            pltpu.VMEM(q.shape, q.dtype), pltpu.VMEM(do.shape, do.dtype), pltpu.SemaphoreType.DMA((4,)),
+        ] + scratch(width, value, ranges),
         compiler_params=pltpu.CompilerParams(vmem_limit_bytes=67043328),
     )(shard, wanted, mask, q, do, latent)
 
@@ -323,7 +423,7 @@
         return self.place.at(-i, -j) if h == 0 else self.place.at(-j, -i)
 
     def rows(self, h, piece=None):
-        return pl.ds(h * 64, 64) if piece is None else pl.ds(h * 64 + piece * 32, 32)
+        return pl.ds(h * 288, 288) if piece is None else pl.ds(h * 288 + piece * 144, 144)
 
     def put(self, h, i, j, second, d, piece=None):
         src = self.full.at[self.source(h, i, j), self.rows(h, piece)]
@@ -568,13 +668,12 @@
     shards = lax.axis_size("ctx")
     shard = lax.axis_index("ctx").astype(jnp.int32)
     mask, wanted = tables(selection, shard, shards)
-    everything = gather(latent, shards).reshape(shards * tok, width)
+    everything = gather(latent.T, shards)
     out, dq, partial = attention(
-        shard[None], wanted, mask, queries.reshape(tok * heads, width),
-        cotangent.reshape(tok * heads, value), everything,
+        shard[None], wanted, mask, queries.transpose(1, 2, 0), cotangent.reshape(tok * heads, value), everything
     )
     grad = reduce_all(partial).T
-    return out.reshape(tok, heads, value), dq.reshape(tok, heads, width), grad
+    return out.reshape(tok, heads, value), dq.transpose(2, 0, 1), grad
 
 
 def solution(mesh):

time: 171 us -> 142 us (0.83)
  Pallas kernels: 151 us -> 133 us
  local copies, waits for them, and re-layouts: 14.9 us -> 3.59 us
    pallas_call x1, Pallas kernels: 86.4 us -> 69.4 us  [reduce_all(): pl.pallas_call(reduce_kernel, out_shape=jax.ShapeDtypeStruct((width, lane...]
    unnamed x6 -> x3, local copies, waits for them, and re-layouts: 14.3 us -> 3.05 us
where the time goes in v2:
time: 142 us; the launch traced here: 141 us
  Pallas kernels  133 us (94%)
  other arithmetic  3.68 us (3%)
  local copies, waits for them, and re-layouts  3.59 us (3%)
    pallas_call x1, Pallas kernels, reduce_all(): pl.pallas_call(reduce_kernel, out_shape=jax.ShapeDtypeStruct((width, lane...  69.4 us
    pallas_call x1, Pallas kernels, attention(): pl.pallas_call(attention_kernel, out_shape=(jax.ShapeDtypeStruct((heads *...  36 us
    pallas_call x1, Pallas kernels, gather(): pl.pallas_call(gather_kernel, out_shape=jax.ShapeDtypeStruct((shards,) +...  28.1 us
    unnamed x3, local copies, waits for them, and re-layouts  3.05 us

profile of v2, /device:TPU:0, one launch (start us, length us, event | category | flops | bytes accessed | tf_op | source)
XLA Modules:
  0.0 141.4 jit_solution(17382100988688157282)
XLA Ops:
  0.6 0.7 compare_reduce_fusion
  1.4 0.1 pad.2.clone
  1.5 0.9 fusion
  2.3 0.1 copy.21
  2.5 0.1 reduce_or.38
  2.5 0.1 copy.19
  2.7 0.7 select_convert_fusion.mask
  3.4 0.1 reshape.31
  3.5 0.6 slice_reduce_fusion
  4.1 0.1 copy.18
  4.2 0.7 select_convert_fusion.1.wanted
  4.9 28.1 %shard_map.67.latent = bf16[32,576,128]{2,1,0:T(8,128)(2,1)} custom-call(bf16[576,128]{1,0:T(8,128)(2,1)} %bitcast.17), custom_call_target="tpu_custom_call" | custom-call | tf_op jit(solution)/shard_map/pallas_call | solution.py:518
  33.0 36.0 %shard_map.68 = (bf16[2048,512]{1,0:T(8,128)(2,1)}, bf16[16,576,128]{2,1,0:T(8,128)(2,1)}, bf16[32,576,128]{2,1,0:T(8,128)(2,1)}) custom-call(s32[1]{0:T(128)} %bitcast.me_ref, s32[2,32]{1,0:T(2,128)} %select_convert_fusion.1.wanted, bf16[128,64]{1,0:T(8,128)(2,1)} %select_convert_fusion.mask, bf16[16,576,128]{2,1,0:T(8,128)(2,1)} %bitcast.15, ...), custom_call_target="tpu_custom_call" | custom-call | tf_op jit(solution)/shard_map/pallas_call | solution.py:334
  69.0 0.0 copy-start
  69.0 2.3 %copy-done = bf16[32,576,128]{2,1,0:T(8,128)(2,1)S(1)} copy-done((bf16[32,576,128]{2,1,0:T(8,128)(2,1)S(1)}, bf16[32,576,128]{2,1,0:T(8,128)(2,1)}, u32[]{:S(2)}) %copy-start) | copy-done | bytes 4718616
  71.3 69.4 %shard_map.69 = f32[576,128]{1,0:T(8,128)S(1)} custom-call(bf16[4,4,2,576,128]{4,3,2,1,0:T(8,128)(2,1)S(1)} %bitcast.13), custom_call_target="tpu_custom_call" | custom-call | tf_op jit(solution)/shard_map/pallas_call | solution.py:637
  140.7 0.7 copy.23
  (5 shorter events, 0.0 us)
Async XLA Ops:
  69.0 2.3 %copy-start = (bf16[32,576,128]{2,1,0:T(8,128)(2,1)S(1)}, bf16[32,576,128]{2,1,0:T(8,128)(2,1)}, u32[]{:S(2)}) copy-start(bf16[32,576,128]{2,1,0:T(8,128)(2,1)} %get-tuple-element.8) | copy-start | bytes 14155780

commit v3 on v2

--- a/solution.py
+++ b/solution.py
@@ -266,87 +266,6 @@
     ]
 
 
-def attention_kernel(me_ref, wanted, mask, q_in, do_in, latent, out_hbm, dq_hbm, dlat, q, do, sems, *refs):
-    shard = me_ref[0]
-    plane = shard // PLANE
-    width = q.shape[1]
-    out, dq = do, q
-    a = Attention(shard, wanted, width, do.shape[1], refs)
-    get_q = pltpu.make_async_copy(q_in, q, sems.at[0])
-    get_do = pltpu.make_async_copy(do_in, do, sems.at[1])
-    put_out = pltpu.make_async_copy(out, out_hbm, sems.at[2])
-    put_dq = pltpu.make_async_copy(dq, dq_hbm, sems.at[3])
-    get_q.start()
-    get_do.start()
-    get_q.wait()
-    get_do.wait()
-
-    def each(count, step):
-        def body(g, carry):
-            step(g)
-            return carry
-
-        lax.fori_loop(0, count, body, 0)
-
-    a.load_queries(q, mask)
-    a.load_cotangent(do)
-    each(plane + 1, lambda g: a.pick(latent, g))
-    a.pick_own(latent[shard])
-    for b in range(2):
-        a.scores(plane, b, True)
-        each(plane, lambda g, b=b: a.scores(g, b, False))
-        a.softmax_start(b)
-        each(plane + 1, lambda g, b=b: a.softmax(g, b))
-        a.softmax_end(b, out)
-    put_out.start()
-    a.grads_extra()
-
-    def grads(g):
-        a.grads(g)
-        for m in range(PLANE // 2):
-            even, odd = a.spread(g, m)
-            j = g * PLANE + 2 * m
-            dlat[j] = even.astype(dlat.dtype)
-            dlat[j + 1] = odd.astype(dlat.dtype)
-
-    def empty(j, carry):
-        dlat[j] = jnp.zeros(dlat.shape[1:], dlat.dtype)
-        return carry
-
-    each(plane + 1, grads)
-    lax.fori_loop((plane + 1) * PLANE, dlat.shape[0], empty, 0)
-    dlat[shard, :, :BLOCK] = (dlat[shard, :, :BLOCK].astype(jnp.float32) + a.accx[...]).astype(dlat.dtype)
-    a.grad_queries_start()
-    each(plane + 1, a.grad_queries)
-    a.grad_queries_end(dq)
-    put_dq.start()
-    put_dq.wait()
-    put_out.wait()
-
-
-def attention(shard, wanted, mask, q, do, latent):
-    heads, width, tok = q.shape
-    value = do.shape[1]
-    ranges = latent.shape[0]
-    vmem = pl.BlockSpec(memory_space=pltpu.VMEM)
-    smem = pl.BlockSpec(memory_space=pltpu.SMEM)
-    hbm = pl.BlockSpec(memory_space=pl.ANY)
-    return pl.pallas_call(
-        attention_kernel,
-        out_shape=(
-            jax.ShapeDtypeStruct((heads * tok, value), jnp.bfloat16),
-            jax.ShapeDtypeStruct((heads, width, tok), jnp.bfloat16),
-            jax.ShapeDtypeStruct((ranges, width, tok), jnp.bfloat16),
-        ),
-        in_specs=[smem, smem, vmem, hbm, hbm, vmem],
-        out_specs=(hbm, hbm, vmem),
-        scratch_shapes=[
-            pltpu.VMEM(q.shape, q.dtype), pltpu.VMEM(do.shape, do.dtype), pltpu.SemaphoreType.DMA((4,)),
-        ] + scratch(width, value, ranges),
-        compiler_params=pltpu.CompilerParams(vmem_limit_bytes=67043328),
-    )(shard, wanted, mask, q, do, latent)
-
-
 def tables(chosen, shard, shards):
     tok = chosen.shape[0]
     picked = jnp.any(chosen[:, :, None] == jnp.arange(2 * shards, dtype=jnp.int32)[None, None, :], axis=1)
@@ -481,48 +400,15 @@
             for h in range(2):
                 self.relay(h, i)
 
-    def last(self):
-        for i in (0, 1, 3, 2):
-            for h in range(2):
-                self.got(h, i, 2)
-                self.trade(h, i, 2)
-
-    def traded(self):
-        for i in range(4):
-            for j in range(4):
-                for h in range(2):
-                    src = self.source(h, i, j) + 1 - 2 * self.place.c
-                    self.wire.wait(self.full.at[src, self.rows(h)], self.twin_recv.at[h, i * 4 + j], self.place.twin())
-
-
-def gather_kernel(own, full, sends, recv, twin_recv, local):
-    place = Place()
-    mine = pltpu.make_async_copy(own, full.at[place.idx], local)
-    mine.start()
-    greet([place.near(0, 1), place.near(0, -1), place.near(1, 1), place.near(1, -1), place.twin()])
-    mine.wait()
-    wire = Wire(sends)
-    g = Gather(place, wire, full, recv, twin_recv)
-    g.start()
-    g.first()
-    g.second()
-    g.third()
-    g.last()
-    g.traded()
-    wire.finish()
-
-
-def gather(latent, shards):
-    vmem = pl.BlockSpec(memory_space=pltpu.VMEM)
-    dma = pltpu.SemaphoreType.DMA
-    return pl.pallas_call(
-        gather_kernel,
-        out_shape=jax.ShapeDtypeStruct((shards,) + latent.shape, latent.dtype),
-        in_specs=[vmem],
-        out_specs=vmem,
-        scratch_shapes=[dma((72,)), dma((2, 16, 2)), dma((2, 16)), dma],
-        compiler_params=pltpu.CompilerParams(collective_id=0, has_side_effects=True),
-    )(latent)
+    def far(self, h, i):
+        self.got(h, i, 2)
+        self.trade(h, i, 2)
+
+    def ready(self, k):
+        for n in range(4):
+            for h, i, j in ((0, k, n), (1, n, k)):
+                src = self.source(h, i, j) + 1 - 2 * self.place.c
+                self.wire.wait(self.full.at[src, self.rows(h)], self.twin_recv.at[h, i * 4 + j], self.place.twin())
 
 
 class Ring:
@@ -554,112 +440,194 @@
         return mine + (self.near[0].astype(jnp.float32) + self.near[1].astype(jnp.float32))
 
 
-LOW = pl.ds(0, 288)
-HIGH = pl.ds(288, 288)
 PIECES = (pl.ds(0, 144), pl.ds(144, 144))
-
-
-def reduce_kernel(
-    part, out, twin_in, sum_a, sum_b, tot_a, tot_b, head_in, head_out, result,
+A_ROWS = pl.ds(0, 288)
+B_ROWS = pl.ds(288, 288)
+
+
+def kernel(
+    wanted, mask, q_in, do_in, latent, out_hbm, dq_hbm, grad,
+    q, do, full, mine, theirs, twin_in, tot_a, tot_b, head_in, head_out, result,
     far_ax, near_ax, far_az, near_az, far_bz, near_bz, far_bx, near_bx,
-    sends, twin_sem, sem_ax, sem_az, sem_bz, sem_bx, sem_y,
+    local, sends, recv, twin_recv, twin_sem, sem_ax, sem_az, sem_bz, sem_bx, sem_y, *refs
 ):
     place = Place()
     z, x, c, y = place.z, place.x, place.c, place.y
+    width = latent.shape[0]
+    a = Attention(place.idx, wanted, width, do.shape[1], refs)
+    out, dq = do, q
+    get_q = pltpu.make_async_copy(q_in, q, local.at[0])
+    get_do = pltpu.make_async_copy(do_in, do, local.at[1])
+    put_out = pltpu.make_async_copy(out, out_hbm, local.at[2])
+    put_dq = pltpu.make_async_copy(dq, dq_hbm, local.at[3])
+    own = pltpu.make_async_copy(latent, full.at[place.idx], local.at[4])
+    own.start()
+    get_q.start()
+    get_do.start()
     others = [{"head": ring(y, d)} for d in (1, 2, 3)]
     greet([place.near(0, 1), place.near(0, -1), place.near(1, 1), place.near(1, -1), place.twin()] + others)
+    own.wait()
     wire = Wire(sends)
+
+    def each(count, step):
+        def body(g, carry):
+            step(g)
+            return carry
+
+        lax.fori_loop(0, count, body, 0)
+
+    g = Gather(place, wire, full, recv, twin_recv)
+    g.start()
+    get_q.wait()
+    a.load_queries(q, mask)
+    g.first()
+    get_do.wait()
+    a.load_cotangent(do)
+    g.second()
+    g.far(0, 0)
+    g.ready(0)
+    a.pick(full, z)
+    a.pick_own(full[place.idx])
+    a.scores(z, 0, True)
+    g.third()
+    g.far(0, 1)
+    g.far(0, 3)
+    for k in (1, 3):
+        g.ready(k)
+
+    def follow(k):
+        plane = ring(z, -k)
+
+        @pl.when(plane < z)
+        def _():
+            a.pick(full, plane)
+            a.scores(plane, 0, False)
+
+    g.far(0, 2)
+    for i in (0, 1, 3, 2):
+        g.far(1, i)
+    follow(1)
+    follow(3)
+    g.ready(2)
+    follow(2)
+    for b in range(2):
+        if b == 1:
+            a.scores(z, b, True)
+            each(z, lambda g: a.scores(g, 1, False))
+        a.softmax_start(b)
+        each(z + 1, lambda g, b=b: a.softmax(g, b))
+        a.softmax_end(b, out)
+    put_out.start()
+    a.grads_extra()
+
     order = [ring(z, 2), ring(z, 1), ring(z, -1), z]
-    for n, g in enumerate(order):
-        wire.send(part.at[g, :, 1 - c], twin_in.at[g], twin_sem.at[g], place.twin())
+
+    def make(g, last):
+        @pl.when(g <= z)
+        def _():
+            a.grads(g)
+            for m in range(4):
+                even, odd = a.spread(g, m)
+                mine[g, m] = jnp.where(c == 0, even, odd).astype(mine.dtype)
+                theirs[g, m] = jnp.where(c == 0, odd, even).astype(mine.dtype)
+
+        if last:
+            mine[g, x, :, :BLOCK] = (mine[g, x, :, :BLOCK].astype(jnp.float32) + a.accx[...]).astype(mine.dtype)
+        else:
+            @pl.when(g > z)
+            def _():
+                for m in range(4):
+                    mine[g, m] = jnp.zeros(mine.shape[2:], mine.dtype)
+                    theirs[g, m] = jnp.zeros(mine.shape[2:], mine.dtype)
+
+        wire.send(theirs.at[g], twin_in.at[g], twin_sem.at[g], place.twin())
+
+    def join(g):
+        wire.wait(twin_in.at[g], twin_sem.at[g], place.twin())
+        for m in range(4):
+            mine[g, m] = (mine[g, m].astype(jnp.float32) + twin_in[g, m].astype(jnp.float32)).astype(mine.dtype)
+
+    a_rings = [
+        Ring(
+            place, wire, 1, lambda t, g=g: mine.at[g, t, A_ROWS], PIECES,
+            far_ax.at[g], near_ax.at[g], sem_ax.at[g, 0], sem_ax.at[g, 1],
+        )
+        for g in order
+    ]
     b_ring = Ring(
-        place, wire, 0, lambda t: sum_b.at[t], (pl.ds(0, 2), pl.ds(2, 2)), far_bz, near_bz, sem_bz.at[0], sem_bz.at[1]
+        place, wire, 0, lambda t: mine.at[t, :, B_ROWS], (pl.ds(0, 2), pl.ds(2, 2)), far_bz, near_bz, sem_bz.at[0], sem_bz.at[1]
     )
-    a_rings = []
-    for n, g in enumerate(order):
-        wire.wait(twin_in.at[g], twin_sem.at[g], place.twin())
-        for k in range(4):
-            both = part[g, k, c].astype(jnp.float32) + twin_in[g, k].astype(jnp.float32)
-            both = both.astype(part.dtype)
-            sum_a[g, k] = both[:288]
-            sum_b[g, k] = both[288:]
-        a_ring = Ring(
-            place, wire, 1, lambda t, g=g: sum_a.at[g, t], PIECES, far_ax.at[g], near_ax.at[g], sem_ax.at[g, 0], sem_ax.at[g, 1]
-        )
-        a_ring.start()
-        if n == 0:
-            b_ring.start()
-        if n == 2:
-            b_ring.middle()
-        if n > 0:
-            a_rings[n - 1].middle()
-        a_rings.append(a_ring)
+    a_last = Ring(place, wire, 0, lambda t: tot_a.at[t], PIECES, far_az, near_az, sem_az.at[0], sem_az.at[1])
+    b_last = Ring(place, wire, 1, lambda t: tot_b.at[t], PIECES, far_bx, near_bx, sem_bx.at[0], sem_bx.at[1])
+
+    def settle(n):
+        tot_a[order[n]] = a_rings[n].total().astype(tot_a.dtype)
+
+    make(order[0], False)
+    make(order[1], False)
+    join(order[0])
+    b_ring.start()
+    a_rings[0].start()
+    make(order[2], False)
+    join(order[1])
+    a_rings[1].start()
+    a_rings[0].middle()
+    make(order[3], True)
+    join(order[2])
+    b_ring.middle()
+    a_rings[2].start()
+    a_rings[1].middle()
+    settle(0)
+    a_last.start()
+    put_out.wait()
+    a.grad_queries_start()
+
+    def queries(n):
+        if n == 3:
+            a.grad_queries(order[n])
+            return
+
+        @pl.when(order[n] < z)
+        def _():
+            a.grad_queries(order[n])
+
+    join(order[3])
+    a_rings[3].start()
+    a_rings[2].middle()
+    settle(1)
+    queries(0)
+    tot_b[...] = b_ring.total().astype(tot_b.dtype)
+    b_last.start()
     a_rings[3].middle()
-    tot_b[...] = b_ring.total().astype(tot_b.dtype)
-    b_last = Ring(place, wire, 1, lambda t: tot_b.at[t], PIECES, far_bx, near_bx, sem_bx.at[0], sem_bx.at[1])
-    b_last.start()
-    a_last = Ring(place, wire, 0, lambda t: tot_a.at[t], PIECES, far_az, near_az, sem_az.at[0], sem_az.at[1])
-    for n, g in enumerate(order):
-        tot_a[g] = a_rings[n].total().astype(tot_a.dtype)
-        if n == 0:
-            a_last.start()
-        if n == 2:
-            a_last.middle()
+    settle(2)
+    a_last.middle()
+    queries(1)
+    settle(3)
     b_last.middle()
+    queries(2)
     low = a_last.total().astype(jnp.bfloat16)
     high = b_last.total().astype(jnp.bfloat16)
-    for q in range(2):
-        head_out[q] = low[q * 144:(q + 1) * 144]
-        head_out[q + 2] = high[q * 144:(q + 1) * 144]
+    for n in range(2):
+        head_out[n] = low[n * 144:(n + 1) * 144]
+        head_out[n + 2] = high[n * 144:(n + 1) * 144]
     for d in (1, 2, 3):
-        t = ring(y, d)
-        wire.send(head_out.at[t], head_in.at[d - 1], sem_y.at[0, d - 1], others[d - 1])
+        wire.send(head_out.at[ring(y, d)], head_in.at[d - 1], sem_y.at[0, d - 1], others[d - 1])
+    queries(3)
     for d in (1, 2, 3):
         wire.wait(head_in.at[d - 1], sem_y.at[0, d - 1], others[d - 1])
-    mine = head_out[y].astype(jnp.float32) + head_in[0].astype(jnp.float32)
-    mine = mine + (head_in[1].astype(jnp.float32) + head_in[2].astype(jnp.float32))
-    result[y] = mine.astype(jnp.bfloat16)
+    total = head_out[y].astype(jnp.float32) + head_in[0].astype(jnp.float32)
+    total = total + (head_in[1].astype(jnp.float32) + head_in[2].astype(jnp.float32))
+    result[y] = total.astype(jnp.bfloat16)
     for d in (1, 2, 3):
         wire.send(result.at[y], result.at[y], sem_y.at[1, d - 1], others[d - 1])
+    a.grad_queries_end(dq)
+    put_dq.start()
     for d in (1, 2, 3):
         wire.wait(result.at[ring(y, -d)], sem_y.at[1, d - 1], others[d - 1])
-    for q in range(4):
-        out[q * 144:(q + 1) * 144, :] = result[q].astype(jnp.float32)
+    for n in range(4):
+        grad[n * 144:(n + 1) * 144, :] = result[n].astype(jnp.float32)
+    put_dq.wait()
     wire.finish()
-
-
-def reduce_all(part):
-    ranges, width, lanes = part.shape
-    vmem = pl.BlockSpec(memory_space=pltpu.VMEM)
-    dma = pltpu.SemaphoreType.DMA
-    low = jnp.bfloat16
-    half, piece = width // 2, width // 4
-    return pl.pallas_call(
-        reduce_kernel,
-        out_shape=jax.ShapeDtypeStruct((width, lanes), jnp.float32),
-        in_specs=[vmem],
-        out_specs=vmem,
-        scratch_shapes=[
-            pltpu.VMEM((4, 4, width, lanes), low),
-            pltpu.VMEM((4, 4, half, lanes), low),
-            pltpu.VMEM((4, 4, half, lanes), low),
-            pltpu.VMEM((4, half, lanes), low),
-            pltpu.VMEM((4, half, lanes), low),
-            pltpu.VMEM((3, piece, lanes), low),
-            pltpu.VMEM((4, piece, lanes), low),
-            pltpu.VMEM((4, piece, lanes), low),
-            pltpu.VMEM((4, 2, piece, lanes), low),
-            pltpu.VMEM((4, 2, half, lanes), low),
-            pltpu.VMEM((2, piece, lanes), low),
-            pltpu.VMEM((2, half, lanes), low),
-            pltpu.VMEM((2, 2, half, lanes), low),
-            pltpu.VMEM((2, 4, half, lanes), low),
-            pltpu.VMEM((2, piece, lanes), low),
-            pltpu.VMEM((2, half, lanes), low),
-            dma((40,)), dma((4,)), dma((4, 2, 2)), dma((2, 2)), dma((2, 2)), dma((2, 2)), dma((2, 3)),
-        ],
-        compiler_params=pltpu.CompilerParams(collective_id=1, has_side_effects=True, vmem_limit_bytes=32 << 20),
-    )(part.reshape(4, 4, 2, width, lanes))
 
 
 def body(queries, latent, cotangent, selection):
@@ -668,12 +636,47 @@
     shards = lax.axis_size("ctx")
     shard = lax.axis_index("ctx").astype(jnp.int32)
     mask, wanted = tables(selection, shard, shards)
-    everything = gather(latent.T, shards)
-    out, dq, partial = attention(
-        shard[None], wanted, mask, queries.transpose(1, 2, 0), cotangent.reshape(tok * heads, value), everything
-    )
-    grad = reduce_all(partial).T
-    return out.reshape(tok, heads, value), dq.transpose(2, 0, 1), grad
+    vmem = pl.BlockSpec(memory_space=pltpu.VMEM)
+    smem = pl.BlockSpec(memory_space=pltpu.SMEM)
+    hbm = pl.BlockSpec(memory_space=pl.ANY)
+    dma = pltpu.SemaphoreType.DMA
+    low = jnp.bfloat16
+    half, piece = width // 2, width // 4
+    out, dq, grad = pl.pallas_call(
+        kernel,
+        out_shape=(
+            jax.ShapeDtypeStruct((heads * tok, value), low),
+            jax.ShapeDtypeStruct((heads, width, tok), low),
+            jax.ShapeDtypeStruct((width, tok), jnp.float32),
+        ),
+        in_specs=[smem, vmem, hbm, hbm, vmem],
+        out_specs=(hbm, hbm, vmem),
+        scratch_shapes=[
+            pltpu.VMEM((heads, width, tok), low),
+            pltpu.VMEM((heads * tok, value), low),
+            pltpu.VMEM((shards, width, tok), low),
+            pltpu.VMEM((4, 4, width, tok), low),
+            pltpu.VMEM((4, 4, width, tok), low),
+            pltpu.VMEM((4, 4, width, tok), low),
+            pltpu.VMEM((4, half, tok), low),
+            pltpu.VMEM((4, half, tok), low),
+            pltpu.VMEM((3, piece, tok), low),
+            pltpu.VMEM((4, piece, tok), low),
+            pltpu.VMEM((4, piece, tok), low),
+            pltpu.VMEM((4, 2, piece, tok), low),
+            pltpu.VMEM((4, 2, half, tok), low),
+            pltpu.VMEM((2, piece, tok), low),
+            pltpu.VMEM((2, half, tok), low),
+            pltpu.VMEM((2, 2, half, tok), low),
+            pltpu.VMEM((2, 4, half, tok), low),
+            pltpu.VMEM((2, piece, tok), low),
+            pltpu.VMEM((2, half, tok), low),
+            dma((5,)), dma((112,)), dma((2, 16, 2)), dma((2, 16)),
+            dma((4,)), dma((4, 2, 2)), dma((2, 2)), dma((2, 2)), dma((2, 2)), dma((2, 3)),
+        ] + scratch(width, value, shards),
+        compiler_params=pltpu.CompilerParams(collective_id=0, has_side_effects=True, vmem_limit_bytes=67043328),
+    )(wanted, mask, queries.transpose(1, 2, 0), cotangent.reshape(tok * heads, value), latent.T)
+    return out.reshape(tok, heads, value), dq.transpose(2, 0, 1), grad.T
 
 
 def solution(mesh):

time: 142 us -> 113 us (0.80)
  Pallas kernels: 133 us -> 102 us
  local copies, waits for them, and re-layouts: 3.59 us -> 5.9 us
    pallas_call x3 -> x1, Pallas kernels: 133 us -> 102 us  [body(): pl.pallas_call(kernel, out_shape=(jax.ShapeDtypeStruct((heads * tok, valu...]
    unnamed x3 -> x7, local copies, waits for them, and re-layouts: 3.05 us -> 5.36 us
where the time goes in v3:
time: 113 us
  Pallas kernels  102 us (90%)
  local copies, waits for them, and re-layouts  5.9 us (5%)
  other arithmetic  3.65 us (3%)
    pallas_call x1, Pallas kernels, body(): pl.pallas_call(kernel, out_shape=(jax.ShapeDtypeStruct((heads * tok, valu...  102 us
    unnamed x7, local copies, waits for them, and re-layouts  5.36 us

profile of v3, /device:TPU:0, one launch (start us, length us, event | category | flops | bytes accessed | tf_op | source)
XLA Modules:
  0.0 112.5 jit_solution(14668708149555617573)
XLA Ops:
  0.6 0.7 compare_reduce_fusion
  1.4 0.1 pad.2.clone
  1.5 0.9 fusion
  2.3 0.1 copy.21
  2.5 0.1 reduce_or.38
  2.5 0.1 copy.19
  2.7 0.7 select_convert_fusion.mask
  3.4 0.1 reshape.28
  3.5 0.6 slice_reduce_fusion
  4.1 0.1 copy.18
  4.2 0.6 select_convert_fusion.1.wanted
  4.9 102.3 %shard_map.67 = (bf16[2048,512]{1,0:T(8,128)(2,1)}, bf16[16,576,128]{2,1,0:T(8,128)(2,1)}, f32[576,128]{1,0:T(8,128)}) custom-call(s32[2,32]{1,0:T(2,128)} %select_convert_fusion.1.wanted, bf16[128,64]{1,0:T(8,128)(2,1)} %select_convert_fusion.mask, bf16[16,576,128]{2,1,0:T(8,128)(2,1)} %bitcast.11, bf16[2048,512]{1,0:T(8,128)(2,1)} %bitcast.13, ...), custom_call_target="tpu_custom_call" | custom-call | tf_op jit(solution)/shard_map/pallas_call | solution.py:645
  107.2 0.0 copy-start
  107.2 3.2 %copy.25 = bf16[128,16,512]{2,1,0:T(8,128)(2,1)} copy(bf16[128,16,512]{2,1,0:T(8,128)(2,1)} %bitcast.14) | data formatting | bytes 4194304
  110.4 0.0 copy-done
  110.4 0.0 copy-start.1
  110.4 1.4 %copy.26 = bf16[128,16,576]{0,2,1:T(8,128)(2,1)} copy(bf16[128,16,576]{0,2,1:T(8,128)(2,1)S(1)} %bitcast.12) | data formatting | bytes 4718592
  111.8 0.0 copy-done.1
  111.8 0.7 copy.27
  (5 shorter events, 0.0 us)
Async XLA Ops:
  107.2 3.2 %copy-start = (bf16[16,576,128]{2,1,0:T(8,128)(2,1)S(1)}, bf16[16,576,128]{2,1,0:T(8,128)(2,1)}, u32[]{:S(2)}) copy-start(bf16[16,576,128]{2,1,0:T(8,128)(2,1)} %get-tuple-element.7) | copy-start | bytes 7077892
  110.4 1.4 %copy-start.1 = (f32[576,128]{1,0:T(8,128)S(1)}, f32[576,128]{1,0:T(8,128)}, u32[]{:S(2)}) copy-start(f32[576,128]{1,0:T(8,128)} %get-tuple-element.8) | copy-start | bytes 884740

commit v4 on v3

--- a/solution.py
+++ b/solution.py
@@ -53,7 +53,7 @@
                 at = pl.ds(pl.multiple_of(b * HALF + m * 128, 128), 128)
                 self.qt[:, at] = x
                 self.qx[at, :width] = x.T
-                bias = mask[b * BLOCK:(b + 1) * BLOCK, :]
+                bias = mask[b * BLOCK:(b + 1) * BLOCK, :].astype(jnp.bfloat16)
                 self.qx[at, width:] = jnp.concatenate([bias, bias], axis=0)
             return carry
 
@@ -153,45 +153,33 @@
         def tile(t, carry):
             r = pl.ds(pl.multiple_of(b * HALF + t * 256, 256), 256)
             inv = 1.0 / jnp.sum(self.arow[r, :], axis=1, keepdims=True)
-            full = self.wide[r, :] * inv
-            self.wide[r, :] = full
+            low = (self.wide[r, :] * inv).astype(jnp.bfloat16)
+            out[r, :] = low
             do = self.do[r, :].astype(jnp.float32)
-            delta = jnp.sum(do * full.astype(jnp.bfloat16).astype(jnp.float32), axis=1, keepdims=True)
+            delta = jnp.sum(do * low.astype(jnp.float32), axis=1, keepdims=True)
             self.dot_t[:, r] = (do * inv).astype(jnp.bfloat16).T
             self.arow[r, :] = jnp.broadcast_to(inv * SCALE, (256, 128))
             self.drow[r, :] = jnp.broadcast_to(inv * SCALE * delta, (256, 128))
             return carry
 
         lax.fori_loop(0, HALF // 256, tile, 0)
-        for k in range(self.value // 128):
-            lanes = slice(k * 128, (k + 1) * 128)
-            self.mrow[self.block(b), :] = self.wide[self.block(b), lanes]
-
-            def token(t, carry, lanes=lanes):
-                at = pl.ds(pl.multiple_of((b * BLOCK + t) * HEADS, HEADS), HEADS)
-                out[at, lanes] = self.mrow[pl.ds(b * HALF + t, HEADS, stride=BLOCK), :].astype(jnp.bfloat16)
-                return carry
-
-            lax.fori_loop(0, BLOCK, token, 0, unroll=8)
-
     def acc(self, b, at):
         return self.s.at[2 + b, at]
 
-    def grads(self, g):
+    def grads(self, g, b):
         value, width = self.value, self.width
-        for b in range(2):
-            r = self.block(b)
-            top, rest = self.acc(b, slice(0, value)), self.acc(b, slice(value, width))
-            top[...] = dot(self.dot_t[:, r], self.p[g, r, :], NN)
-            self.s[b] = dot(self.do[r, :], self.ksel[b, self.keys(g), :value], NT)
-            for k in range(KEYS // 128):
-                lanes = slice(k * 128, (k + 1) * 128)
-                e = self.p[g, r, lanes].astype(jnp.float32)
-                d = e * (self.s[b, :, lanes] * self.arow[r, :] - self.drow[r, :])
-                self.p[g, r, lanes] = d.astype(jnp.bfloat16)
-            dk = dot(self.qt[:, r], self.p[g, r, :], NN)
-            top[...] += dk[:value]
-            rest[...] = dk[value:]
+        r = self.block(b)
+        top, rest = self.acc(b, slice(0, value)), self.acc(b, slice(value, width))
+        top[...] = dot(self.dot_t[:, r], self.p[g, r, :], NN)
+        self.s[b] = dot(self.do[r, :], self.ksel[b, self.keys(g), :value], NT)
+        for k in range(KEYS // 128):
+            lanes = slice(k * 128, (k + 1) * 128)
+            e = self.p[g, r, lanes].astype(jnp.float32)
+            d = e * (self.s[b, :, lanes] * self.arow[r, :] - self.drow[r, :])
+            self.p[g, r, lanes] = d.astype(jnp.bfloat16)
+        dk = dot(self.qt[:, r], self.p[g, r, :], NN)
+        top[...] += dk[:value]
+        rest[...] = dk[value:]
 
     def grads_extra(self):
         value, r = self.value, self.block(1)
@@ -267,16 +255,16 @@
 
 
 def tables(chosen, shard, shards):
-    tok = chosen.shape[0]
-    picked = jnp.any(chosen[:, :, None] == jnp.arange(2 * shards, dtype=jnp.int32)[None, None, :], axis=1)
-    grouped = picked.reshape(tok, shards, 2)
-    mine = jnp.arange(shards, dtype=jnp.int32) == shard
-    per_range = jnp.any(grouped, axis=2) | mine[None, :]
-    first = jnp.any(chosen == 2 * shard, axis=1)
-    allowed = jnp.concatenate([per_range, first[:, None], jnp.ones((tok, 31), bool)], axis=1)
-    mask = jnp.where(allowed, 0.0, -BIG).astype(jnp.bfloat16)
-    second = jnp.any(picked.reshape(2, BLOCK, shards, 2)[..., 1], axis=1)
-    wanted = jnp.where(mine[None, :], jnp.arange(2)[:, None] == 1, second).astype(jnp.int32)
+    tok, picks = chosen.shape
+    column = jnp.arange(64, dtype=jnp.int32)[None, None, :]
+    listed = chosen[:, :, None]
+    hit = (listed >> 1 == column) | (column == shards) & (listed == 2 * shard) | (column > shards)
+    mask = jnp.max(jnp.where(hit, 0.0, -BIG), axis=1)
+    half = chosen.reshape(2, tok // 2, picks, 1)
+    ranges = jnp.arange(shards, dtype=jnp.int32)[None, None, None, :]
+    second = jnp.arange(2, dtype=jnp.int32)[:, None, None, None] == 1
+    hit = jnp.where(ranges == shard, second, half == 2 * ranges + 1)
+    wanted = jnp.max(jnp.where(hit, 1, 0), axis=(1, 2))
     return mask, wanted
 
 
@@ -313,7 +301,7 @@
 
 class Wire:
     def __init__(self, sems):
-        self.sems, self.sent = sems, []
+        self.sems, self.sent, self.done = sems, [], 0
 
     def send(self, src, dst, recv, target):
         copy = pltpu.make_async_remote_copy(
@@ -330,8 +318,9 @@
         ).wait_recv()
 
     def finish(self):
-        for copy in self.sent:
+        for copy in self.sent[self.done:]:
             copy.wait_send()
+        self.done = len(self.sent)
 
 
 class Gather:
@@ -425,8 +414,9 @@
                 self.block(self.to[2]).at[self.halves[k]], self.far.at[k], self.far_sem.at[k], self.place.near(self.axis, d)
             )
 
-    def middle(self):
-        for k, d in ((0, 1), (1, -1)):
+    def middle(self, ways=(0, 1)):
+        for k in ways:
+            d = 1 - 2 * k
             self.wire.wait(self.far.at[k], self.far_sem.at[k], self.place.near(self.axis, -d))
             ref = self.block(self.to[d])
             part = ref[self.halves[k]].astype(jnp.float32) + self.far[k].astype(jnp.float32)
@@ -447,7 +437,7 @@
 
 def kernel(
     wanted, mask, q_in, do_in, latent, out_hbm, dq_hbm, grad,
-    q, do, full, mine, theirs, twin_in, tot_a, tot_b, head_in, head_out, result,
+    q, do, full, mine, twin_in, tot_a, tot_b, head_in, head_out, result,
     far_ax, near_ax, far_az, near_az, far_bz, near_bz, far_bx, near_bx,
     local, sends, recv, twin_recv, twin_sem, sem_ax, sem_az, sem_bz, sem_bx, sem_y, *refs
 ):
@@ -519,17 +509,24 @@
         a.softmax_end(b, out)
     put_out.start()
     a.grads_extra()
+    wire.finish()
 
     order = [ring(z, 2), ring(z, 1), ring(z, -1), z]
 
-    def make(g, last):
+    def make(g, last, meanwhile):
         @pl.when(g <= z)
         def _():
-            a.grads(g)
+            a.grads(g, 0)
+
+        meanwhile()
+
+        @pl.when(g <= z)
+        def _():
+            a.grads(g, 1)
             for m in range(4):
                 even, odd = a.spread(g, m)
                 mine[g, m] = jnp.where(c == 0, even, odd).astype(mine.dtype)
-                theirs[g, m] = jnp.where(c == 0, odd, even).astype(mine.dtype)
+                full[4 * g + m] = jnp.where(c == 0, odd, even).astype(mine.dtype)
 
         if last:
             mine[g, x, :, :BLOCK] = (mine[g, x, :, :BLOCK].astype(jnp.float32) + a.accx[...]).astype(mine.dtype)
@@ -538,9 +535,9 @@
             def _():
                 for m in range(4):
                     mine[g, m] = jnp.zeros(mine.shape[2:], mine.dtype)
-                    theirs[g, m] = jnp.zeros(mine.shape[2:], mine.dtype)
-
-        wire.send(theirs.at[g], twin_in.at[g], twin_sem.at[g], place.twin())
+                    full[4 * g + m] = jnp.zeros(mine.shape[2:], mine.dtype)
+
+        wire.send(full.at[pl.ds(4 * g, 4)], twin_in.at[g], twin_sem.at[g], place.twin())
 
     def join(g):
         wire.wait(twin_in.at[g], twin_sem.at[g], place.twin())
@@ -563,25 +560,6 @@
     def settle(n):
         tot_a[order[n]] = a_rings[n].total().astype(tot_a.dtype)
 
-    make(order[0], False)
-    make(order[1], False)
-    join(order[0])
-    b_ring.start()
-    a_rings[0].start()
-    make(order[2], False)
-    join(order[1])
-    a_rings[1].start()
-    a_rings[0].middle()
-    make(order[3], True)
-    join(order[2])
-    b_ring.middle()
-    a_rings[2].start()
-    a_rings[1].middle()
-    settle(0)
-    a_last.start()
-    put_out.wait()
-    a.grad_queries_start()
-
     def queries(n):
         if n == 3:
             a.grad_queries(order[n])
@@ -591,20 +569,45 @@
         def _():
             a.grad_queries(order[n])
 
+    def during_1():
+        join(order[0])
+        b_ring.start()
+        a_rings[0].start()
+
+    def during_2():
+        join(order[1])
+        b_ring.middle((0,))
+        a_rings[1].start()
+        a_rings[0].middle()
+
+    def during_3():
+        join(order[2])
+        b_ring.middle((1,))
+        a_rings[2].start()
+        a_rings[1].middle()
+        settle(0)
+        a_last.start()
+
+    make(order[0], False, lambda: None)
+    make(order[1], False, during_1)
+    make(order[2], False, during_2)
+    make(order[3], True, during_3)
+    a_rings[2].middle()
+    settle(1)
+    put_out.wait()
+    a.grad_queries_start()
+    queries(0)
     join(order[3])
     a_rings[3].start()
-    a_rings[2].middle()
-    settle(1)
-    queries(0)
     tot_b[...] = b_ring.total().astype(tot_b.dtype)
     b_last.start()
-    a_rings[3].middle()
     settle(2)
     a_last.middle()
     queries(1)
-    settle(3)
+    a_rings[3].middle()
     b_last.middle()
     queries(2)
+    settle(3)
     low = a_last.total().astype(jnp.bfloat16)
     high = b_last.total().astype(jnp.bfloat16)
     for n in range(2):
@@ -657,7 +660,6 @@
             pltpu.VMEM((shards, width, tok), low),
             pltpu.VMEM((4, 4, width, tok), low),
             pltpu.VMEM((4, 4, width, tok), low),
-            pltpu.VMEM((4, 4, width, tok), low),
             pltpu.VMEM((4, half, tok), low),
             pltpu.VMEM((4, half, tok), low),
             pltpu.VMEM((3, piece, tok), low),
@@ -676,6 +678,7 @@
         ] + scratch(width, value, shards),
         compiler_params=pltpu.CompilerParams(collective_id=0, has_side_effects=True, vmem_limit_bytes=67043328),
     )(wanted, mask, queries.transpose(1, 2, 0), cotangent.reshape(tok * heads, value), latent.T)
+    out = out.reshape(2, heads, BLOCK, value).transpose(0, 2, 1, 3)
     return out.reshape(tok, heads, value), dq.transpose(2, 0, 1), grad.T
 
 

time: 113 us -> 104 us (0.920)
  Pallas kernels: 102 us -> 91.4 us
  local copies, waits for them, and re-layouts: 5.9 us -> 7.88 us
    pallas_call x1, Pallas kernels: 102 us -> 91.4 us  [body(): pl.pallas_call(kernel, out_shape=(jax.ShapeDtypeStruct((heads * tok, valu...]
    transpose x0 -> x1, local copies, waits for them, and re-layouts: none -> 4.22 us  [body(): out = out.reshape(2, heads, BLOCK, value).transpose(0, 2, 1, 3)]
    unnamed x7 -> x6, local copies, waits for them, and re-layouts: 5.36 us -> 2.13 us
    reduce_or x4 -> x0, other arithmetic: 2.27 us -> none  [the longest x1 0.85 us: tables(): jnp.any(chosen[:, :, None] == jnp.arange(2 * shards, dtype=jnp.int32)[Non...]
    reduce_max x0 -> x2, other arithmetic: none -> 1.35 us  [the longest x1 1.01 us: tables(): wanted = jnp.max(jnp.where(hit, 1, 0), axis=(1, 2))]
    convert_element_type x2 -> x0, other arithmetic: 1.35 us -> none  [the longest x1 0.71 us: tables(): mask = jnp.where(allowed, 0.0, -BIG).astype(jnp.bfloat16)]
where the time goes in v4:
time: 104 us; the launch traced here: 103 us
  Pallas kernels  91.4 us (88%)
  local copies, waits for them, and re-layouts  7.88 us (8%)
  other arithmetic  2.82 us (3%)
    pallas_call x1, Pallas kernels, body(): pl.pallas_call(kernel, out_shape=(jax.ShapeDtypeStruct((heads * tok, valu...  91.4 us
    transpose x1, local copies, waits for them, and re-layouts, body(): out = out.reshape(2, heads, BLOCK, value).transpose(0, 2, 1, 3)  4.22 us
    unnamed x6, local copies, waits for them, and re-layouts  2.13 us

profile of v4, /device:TPU:0, one launch (start us, length us, event | category | flops | bytes accessed | tf_op | source)
XLA Modules:
  0.0 102.8 jit_solution(2688707642383649569)
XLA Ops:
  0.7 0.7 broadcast_compare_fusion
  1.4 0.7 broadcast_shift-right-arithmetic_fusion
  2.1 0.3 select_reduce_fusion
  2.5 0.7 copy.12.mask
  3.2 0.8 eq.65
  4.0 1.0 select_reduce_fusion.1.wanted
  5.0 91.4 %shard_map.67 = (bf16[2048,512]{1,0:T(8,128)(2,1)}, bf16[16,576,128]{2,1,0:T(8,128)(2,1)}, f32[576,128]{1,0:T(8,128)}) custom-call(s32[2,32]{1,0:T(2,128)} %select_reduce_fusion.1.wanted, f32[128,64]{1,0:T(8,128)} %copy.12.mask, bf16[16,576,128]{2,1,0:T(8,128)(2,1)} %bitcast.11, bf16[2048,512]{1,0:T(8,128)(2,1)} %bitcast.13, bf16[576,128]{1,0:T(8,128)(2,1)} %bitcast.17), custom_call_target="tpu_custom_call" | custom-call | tf_op jit(solution)/shard_map/pallas_call | solution.py:648
  96.5 0.0 copy-start
  96.5 4.2 %copy.13 = bf16[2,64,16,512]{3,2,1,0:T(8,128)(2,1)} copy(bf16[2,64,16,512]{3,1,2,0:T(8,128)(2,1)} %bitcast.15) | data formatting | bytes 4194304 | tf_op jit(solution)/shard_map/transpose | solution.py:681
  100.7 0.0 copy-done
  100.7 0.0 copy-start.1
  100.7 1.4 %copy.16 = bf16[128,16,576]{0,2,1:T(8,128)(2,1)} copy(bf16[128,16,576]{0,2,1:T(8,128)(2,1)S(1)} %bitcast.12) | data formatting | bytes 4718592
  102.1 0.0 copy-done.1
  102.1 0.7 copy.17
  (5 shorter events, 0.0 us)
Async XLA Ops:
  96.5 4.2 %copy-start = (bf16[16,576,128]{2,1,0:T(8,128)(2,1)S(1)}, bf16[16,576,128]{2,1,0:T(8,128)(2,1)}, u32[]{:S(2)}) copy-start(bf16[16,576,128]{2,1,0:T(8,128)(2,1)} %get-tuple-element.7) | copy-start | bytes 7077892
  100.7 1.4 %copy-start.1 = (f32[576,128]{1,0:T(8,128)S(1)}, f32[576,128]{1,0:T(8,128)}, u32[]{:S(2)}) copy-start(f32[576,128]{1,0:T(8,128)} %get-tuple-element.8) | copy-start | bytes 884740

commit v5 on v4

--- a/solution.py
+++ b/solution.py
@@ -2,6 +2,7 @@
 
 import jax
 import jax.numpy as jnp
+import numpy as np
 from jax import lax
 from jax.experimental import pallas as pl
 from jax.experimental.pallas import tpu as pltpu
@@ -33,12 +34,26 @@
         (self.qx, self.qt, self.do, self.dot_t, self.ksel, self.kx, self.s, self.p, self.sx, self.px,
          self.mrow, self.arow, self.drow, self.wide, self.accx) = refs
         self.pad = self.qx.shape[1] - width
+        self.shards = self.ksel.shape[1] // BLOCK
 
     def keys(self, g):
         return pl.ds(pl.multiple_of(g * KEYS, KEYS), KEYS)
 
     def block(self, b):
         return slice(b * HALF, (b + 1) * HALF)
+
+    def second(self, b, j):
+        return jnp.where(j == self.shard, b, self.wanted[b * self.shards + j]) == 1
+
+    def load_mask(self, chosen, mask):
+        column = lax.broadcasted_iota(jnp.int32, mask.shape, 1)
+        bias = jnp.where(column > self.shards, 0.0, -BIG)
+        lists = chosen[...].T
+        for n in range(lists.shape[1]):
+            listed = lists[:, n:n + 1]
+            hit = (listed >> 1 == column) | ((column == self.shards) & (listed == 2 * self.shard))
+            bias = jnp.where(hit, 0.0, bias)
+        mask[...] = bias.astype(mask.dtype)
 
     def load_queries(self, q, mask):
         width = self.width
@@ -53,7 +68,7 @@
                 at = pl.ds(pl.multiple_of(b * HALF + m * 128, 128), 128)
                 self.qt[:, at] = x
                 self.qx[at, :width] = x.T
-                bias = mask[b * BLOCK:(b + 1) * BLOCK, :].astype(jnp.bfloat16)
+                bias = mask[b * BLOCK:(b + 1) * BLOCK, :]
                 self.qx[at, width:] = jnp.concatenate([bias, bias], axis=0)
             return carry
 
@@ -89,7 +104,7 @@
             r0, r1 = swap(k0), swap(k1)
             at = pl.ds(pl.multiple_of(j * BLOCK, 128), 128)
             for b in range(2):
-                w0, w1 = self.wanted[b, j] == 1, self.wanted[b, j + 1] == 1
+                w0, w1 = self.second(b, j), self.second(b, j + 1)
                 x = jnp.where(lower, jnp.where(w0, r0, k0), jnp.where(w1, k1, r1)).astype(jnp.bfloat16)
                 self.ksel[b, at, :width] = x.T
                 self.ksel[b, at, width:] = jnp.where(column == j + slot, 1.0, 0.0).astype(jnp.bfloat16)
@@ -199,8 +214,8 @@
         for b in range(2):
             x = self.acc(b, slice(0, self.width))[:, m * 128:(m + 1) * 128]
             rolled = swap(x)
-            w0 = self.wanted[b, j] == 1
-            w1 = self.wanted[b, j + 1] == 1
+            w0 = self.second(b, j)
+            w1 = self.second(b, j + 1)
             even = even + jnp.where(lower ^ w0, jnp.where(w0, rolled, x), 0.0)
             odd = odd + jnp.where(lower ^ w1, jnp.where(w1, x, rolled), 0.0)
         return even, odd
@@ -254,18 +269,12 @@
     ]
 
 
-def tables(chosen, shard, shards):
-    tok, picks = chosen.shape
-    column = jnp.arange(64, dtype=jnp.int32)[None, None, :]
-    listed = chosen[:, :, None]
-    hit = (listed >> 1 == column) | (column == shards) & (listed == 2 * shard) | (column > shards)
-    mask = jnp.max(jnp.where(hit, 0.0, -BIG), axis=1)
-    half = chosen.reshape(2, tok // 2, picks, 1)
-    ranges = jnp.arange(shards, dtype=jnp.int32)[None, None, None, :]
-    second = jnp.arange(2, dtype=jnp.int32)[:, None, None, None] == 1
-    hit = jnp.where(ranges == shard, second, half == 2 * ranges + 1)
-    wanted = jnp.max(jnp.where(hit, 1, 0), axis=(1, 2))
-    return mask, wanted
+def choices(chosen, shards):
+    token = np.arange(chosen.shape[0], dtype=np.int32)
+    entry = np.arange(2 * shards, dtype=np.int32)
+    mark = chosen + jnp.asarray(token // BLOCK * 128)[:, None]
+    wanted = jnp.asarray(2 * (entry % shards) + 1 + entry // shards * 128)
+    return jnp.max((mark[:, :, None] == wanted[None, None, :]).astype(jnp.int32), axis=(0, 1))
 
 
 MESH_ID = pl.DeviceIdType.MESH
@@ -430,14 +439,15 @@
         return mine + (self.near[0].astype(jnp.float32) + self.near[1].astype(jnp.float32))
 
 
-PIECES = (pl.ds(0, 144), pl.ds(144, 144))
-A_ROWS = pl.ds(0, 288)
-B_ROWS = pl.ds(288, 288)
+A, B = 384, 192
+A_ROWS, B_ROWS = pl.ds(0, A), pl.ds(A, B)
+A_PIECES = (pl.ds(0, A // 2), pl.ds(A // 2, A // 2))
+B_PIECES = (pl.ds(0, B // 2), pl.ds(B // 2, B // 2))
 
 
 def kernel(
-    wanted, mask, q_in, do_in, latent, out_hbm, dq_hbm, grad,
-    q, do, full, mine, twin_in, tot_a, tot_b, head_in, head_out, result,
+    wanted, chosen, q_in, do_in, latent, out_hbm, dq_hbm, grad,
+    mask, q, do, full, mine, twin_in, tot_a, tot_b, head_in, head_out, result,
     far_ax, near_ax, far_az, near_az, far_bz, near_bz, far_bx, near_bx,
     local, sends, recv, twin_recv, twin_sem, sem_ax, sem_az, sem_bz, sem_bx, sem_y, *refs
 ):
@@ -468,6 +478,7 @@
 
     g = Gather(place, wire, full, recv, twin_recv)
     g.start()
+    a.load_mask(chosen, mask)
     get_q.wait()
     a.load_queries(q, mask)
     g.first()
@@ -496,8 +507,7 @@
     g.far(0, 2)
     for i in (0, 1, 3, 2):
         g.far(1, i)
-    follow(1)
-    follow(3)
+    each(2, lambda n: follow(2 * n + 1))
     g.ready(2)
     follow(2)
     for b in range(2):
@@ -546,7 +556,7 @@
 
     a_rings = [
         Ring(
-            place, wire, 1, lambda t, g=g: mine.at[g, t, A_ROWS], PIECES,
+            place, wire, 1, lambda t, g=g: mine.at[g, t, A_ROWS], A_PIECES,
             far_ax.at[g], near_ax.at[g], sem_ax.at[g, 0], sem_ax.at[g, 1],
         )
         for g in order
@@ -554,8 +564,8 @@
     b_ring = Ring(
         place, wire, 0, lambda t: mine.at[t, :, B_ROWS], (pl.ds(0, 2), pl.ds(2, 2)), far_bz, near_bz, sem_bz.at[0], sem_bz.at[1]
     )
-    a_last = Ring(place, wire, 0, lambda t: tot_a.at[t], PIECES, far_az, near_az, sem_az.at[0], sem_az.at[1])
-    b_last = Ring(place, wire, 1, lambda t: tot_b.at[t], PIECES, far_bx, near_bx, sem_bx.at[0], sem_bx.at[1])
+    a_last = Ring(place, wire, 0, lambda t: tot_a.at[t], A_PIECES, far_az, near_az, sem_az.at[0], sem_az.at[1])
+    b_last = Ring(place, wire, 1, lambda t: tot_b.at[t], B_PIECES, far_bx, near_bx, sem_bx.at[0], sem_bx.at[1])
 
     def settle(n):
         tot_a[order[n]] = a_rings[n].total().astype(tot_a.dtype)
@@ -610,9 +620,9 @@
     settle(3)
     low = a_last.total().astype(jnp.bfloat16)
     high = b_last.total().astype(jnp.bfloat16)
-    for n in range(2):
-        head_out[n] = low[n * 144:(n + 1) * 144]
-        head_out[n + 2] = high[n * 144:(n + 1) * 144]
+    both = jnp.concatenate([low, high], axis=0)
+    for n in range(4):
+        head_out[n] = both[n * 144:(n + 1) * 144]
     for d in (1, 2, 3):
         wire.send(head_out.at[ring(y, d)], head_in.at[d - 1], sem_y.at[0, d - 1], others[d - 1])
     queries(3)
@@ -637,14 +647,13 @@
     tok, heads, width = queries.shape
     value = cotangent.shape[2]
     shards = lax.axis_size("ctx")
-    shard = lax.axis_index("ctx").astype(jnp.int32)
-    mask, wanted = tables(selection, shard, shards)
+    wanted = choices(selection, shards)
     vmem = pl.BlockSpec(memory_space=pltpu.VMEM)
     smem = pl.BlockSpec(memory_space=pltpu.SMEM)
     hbm = pl.BlockSpec(memory_space=pl.ANY)
     dma = pltpu.SemaphoreType.DMA
     low = jnp.bfloat16
-    half, piece = width // 2, width // 4
+    piece = width // 4
     out, dq, grad = pl.pallas_call(
         kernel,
         out_shape=(
@@ -655,29 +664,30 @@
         in_specs=[smem, vmem, hbm, hbm, vmem],
         out_specs=(hbm, hbm, vmem),
         scratch_shapes=[
+            pltpu.VMEM((tok, 64), low),
             pltpu.VMEM((heads, width, tok), low),
             pltpu.VMEM((heads * tok, value), low),
             pltpu.VMEM((shards, width, tok), low),
             pltpu.VMEM((4, 4, width, tok), low),
             pltpu.VMEM((4, 4, width, tok), low),
-            pltpu.VMEM((4, half, tok), low),
-            pltpu.VMEM((4, half, tok), low),
+            pltpu.VMEM((4, A, tok), low),
+            pltpu.VMEM((4, B, tok), low),
             pltpu.VMEM((3, piece, tok), low),
             pltpu.VMEM((4, piece, tok), low),
             pltpu.VMEM((4, piece, tok), low),
-            pltpu.VMEM((4, 2, piece, tok), low),
-            pltpu.VMEM((4, 2, half, tok), low),
-            pltpu.VMEM((2, piece, tok), low),
-            pltpu.VMEM((2, half, tok), low),
-            pltpu.VMEM((2, 2, half, tok), low),
-            pltpu.VMEM((2, 4, half, tok), low),
-            pltpu.VMEM((2, piece, tok), low),
-            pltpu.VMEM((2, half, tok), low),
+            pltpu.VMEM((4, 2, A // 2, tok), low),
+            pltpu.VMEM((4, 2, A, tok), low),
+            pltpu.VMEM((2, A // 2, tok), low),
+            pltpu.VMEM((2, A, tok), low),
+            pltpu.VMEM((2, 2, B, tok), low),
+            pltpu.VMEM((2, 4, B, tok), low),
+            pltpu.VMEM((2, B // 2, tok), low),
+            pltpu.VMEM((2, B, tok), low),
             dma((5,)), dma((112,)), dma((2, 16, 2)), dma((2, 16)),
             dma((4,)), dma((4, 2, 2)), dma((2, 2)), dma((2, 2)), dma((2, 2)), dma((2, 3)),
         ] + scratch(width, value, shards),
         compiler_params=pltpu.CompilerParams(collective_id=0, has_side_effects=True, vmem_limit_bytes=67043328),
-    )(wanted, mask, queries.transpose(1, 2, 0), cotangent.reshape(tok * heads, value), latent.T)
+    )(wanted, selection.T, queries.transpose(1, 2, 0), cotangent.reshape(tok * heads, value), latent.T)
     out = out.reshape(2, heads, BLOCK, value).transpose(0, 2, 1, 3)
     return out.reshape(tok, heads, value), dq.transpose(2, 0, 1), grad.T
 

time: 104 us -> 104 us (level)
  Pallas kernels: 91.4 us -> 93.5 us
  local copies, waits for them, and re-layouts: 7.88 us -> 6.35 us
    pallas_call x1, Pallas kernels: 91.4 us -> 93.5 us  [body(): pl.pallas_call(kernel, out_shape=(jax.ShapeDtypeStruct((heads * tok, valu...]
where the time goes in v5:
time: 104 us; the launch traced here: 103 us
  Pallas kernels  93.5 us (90%)
  local copies, waits for them, and re-layouts  6.35 us (6%)
  other arithmetic  2.22 us (2%)
    pallas_call x1, Pallas kernels, body(): pl.pallas_call(kernel, out_shape=(jax.ShapeDtypeStruct((heads * tok, valu...  93.5 us
    transpose x1, local copies, waits for them, and re-layouts, body(): out = out.reshape(2, heads, BLOCK, value).transpose(0, 2, 1, 3)  4.22 us
    unnamed x6, local copies, waits for them, and re-layouts  2.13 us

profile of v5, /device:TPU:0, one launch (start us, length us, event | category | flops | bytes accessed | tf_op | source)
XLA Modules:
  0.0 102.7 jit_solution(9312315973418014862)
XLA Ops:
  0.6 0.7 broadcast_add_fusion
  1.4 1.5 %convert_reduce_fusion.wanted = s32[64]{0:T(128)} fusion(s32[128,32]{0,1:T(8,128)S(1)} %broadcast_add_fusion, s32[64]{0:T(128)} %constant.7.clone), kind=kLoop, calls=%fused_computation | loop fusion | flops 786368 | bytes 16896 | tf_op jit(solution)/shard_map/reduce_max | solution.py:277
  2.8 93.5 %shard_map.85 = (bf16[2048,512]{1,0:T(8,128)(2,1)}, bf16[16,576,128]{2,1,0:T(8,128)(2,1)}, f32[576,128]{1,0:T(8,128)}) custom-call(s32[64]{0:T(128)} %convert_reduce_fusion.wanted, s32[32,128]{1,0:T(8,128)} %bitcast.17, bf16[16,576,128]{2,1,0:T(8,128)(2,1)} %bitcast.10, bf16[2048,512]{1,0:T(8,128)(2,1)} %bitcast.12, bf16[576,128]{1,0:T(8,128)(2,1)} %bitcast.16), custom_call_target="tpu_custom_call" | custom-call | tf_op jit(solution)/shard_map/pallas_call | solution.py:657
  96.3 0.0 copy-start
  96.3 4.2 %copy.11 = bf16[2,64,16,512]{3,2,1,0:T(8,128)(2,1)} copy(bf16[2,64,16,512]{3,1,2,0:T(8,128)(2,1)} %bitcast.14) | data formatting | bytes 4194304 | tf_op jit(solution)/shard_map/transpose | solution.py:691
  100.6 0.0 copy-done
  100.6 0.0 copy-start.1
  100.6 1.4 %copy.14 = bf16[128,16,576]{0,2,1:T(8,128)(2,1)} copy(bf16[128,16,576]{0,2,1:T(8,128)(2,1)S(1)} %bitcast.11) | data formatting | bytes 4718592
  102.0 0.0 copy-done.1
  102.0 0.7 copy.15
Async XLA Ops:
  96.3 4.2 %copy-start = (bf16[16,576,128]{2,1,0:T(8,128)(2,1)S(1)}, bf16[16,576,128]{2,1,0:T(8,128)(2,1)}, u32[]{:S(2)}) copy-start(bf16[16,576,128]{2,1,0:T(8,128)(2,1)} %get-tuple-element.7) | copy-start | bytes 7077892
  100.6 1.4 %copy-start.1 = (f32[576,128]{1,0:T(8,128)S(1)}, f32[576,128]{1,0:T(8,128)}, u32[]{:S(2)}) copy-start(f32[576,128]{1,0:T(8,128)} %get-tuple-element.8) | copy-start | bytes 884740
